TPU v7x, 128 devices: a whole 4x4x4 slice. The times are simulated.
128 devices in a mesh: rep: 8 (over z_lo, x), tp: 16 (over y, z_hi, core).
Axes of the slice: x: 4, y: 4, z: 4 (z_hi: 2, z_lo: 2; z = z_hi * 2 + z_lo), core: 2. Of those that a mesh axis runs over, the one named last changes fastest.
Arguments:
- batch_rows: bfloat16 [12288, 4096], P(('rep', 'tp')), may hold values from -6 to 6
- token_slots: int32 [8, 384], P('rep'), may hold values from 0 to 1535, as said below
- holder_map: int32 [8, 16], P('rep'), may hold values from -2 to 111, as said below
- copies: bfloat16 [32768, 16384], P('rep', 'tp'), may hold values from -6 to 6
- upstream: bfloat16 [3072, 16384], P('rep', 'tp'), may hold values from -18 to 18
- up_act: bfloat16 [3072, 16384], P('rep', 'tp'), may hold values from -6 to 6
- master: float32 [4096, 14336], P('rep', 'tp'), may hold values from -0.078125 to 0.078125
- moment1: bfloat16 [4096, 14336], P('rep', 'tp'), may hold values from -0.75 to 0.75
- moment2: bfloat16 [4096, 14336], P('rep', 'tp'), may hold values from 0.049804688 to 2
Outputs:
- master_next: float32 [4096, 14336], P('rep', 'tp')
- moment1_next: bfloat16 [4096, 14336], P('rep', 'tp')
- moment2_next: bfloat16 [4096, 14336], P('rep', 'tp')
- copy_next: bfloat16 [32768, 16384], P('rep', 'tp')
Inputs may be any that keep to these rules, and one draw needn't show every extreme that they name: `token_slots`: row r lists 384 distinct rows of replica r's batch. `holder_map`: each row is one replica. A row is either -1 everywhere, or holds -2 at exactly 2 devices and at every other device a distinct piece 7 * j + s (0 <= s < 7) with j one of that row's -2 devices, each such piece exactly once. 4 rows are of the second kind. Columns of copies, upstream and up_act that the steps do not name are not read.
All inputs are finite; a program needn't handle non-finite values.
Results may differ from a plain program's by a relative error of at most 0.02.
Values may be sent and summed in bfloat16 or wider, within the bound.
A program may use at most 128 MiB of HBM per device.

v0:
```python
import math

import jax
import jax.numpy as jnp
from jax import lax
from jax.sharding import PartitionSpec as P

beta_one = 0.9
beta_two = 0.95
bias_one = 1.0 - 0.9**10
bias_two = 1.0 - 0.95**10
learn_rate = 0.05
weight_decay = 0.1
epsilon = 1e-08


def from_everyone(array, axis):
    copies = jnp.broadcast_to(array, (lax.axis_size(axis), *array.shape))
    return lax.all_to_all(copies, axis, split_axis=0, concat_axis=0, tiled=True)


def joined_along(pieces, dim):
    shape = list(pieces.shape[1:])
    shape[dim] *= pieces.shape[0]
    return jnp.moveaxis(pieces, 0, dim).reshape(shape)


def gathered_copies(array, axis, dim):
    pieces = from_everyone(array, axis)
    return joined_along(pieces, dim)


def rows_for(lines, count):
    spare = -lines.shape[0] % count
    if not spare:
        return lines
    return jnp.concatenate([lines, jnp.zeros((spare, *lines.shape[1:]), lines.dtype)])


def sum_in_two_steps(array, axis):
    lines = array.reshape(-1, *array.shape[1:][-1:])
    own = lax.psum_scatter(
        rows_for(lines, lax.axis_size(axis)), axis, scatter_dimension=0, tiled=True
    )
    whole = lax.all_gather(own, axis).reshape(-1, *lines.shape[1:])
    return lax.slice_in_dim(whole, 0, len(lines)).reshape(array.shape)


def on_device(
    batch_rows, token_slots, holder_map, copies, upstream, up_act, master, moment1, moment2
):
    tp_count = lax.axis_size("tp")
    position = lax.axis_index("tp")
    chosen = token_slots[0]
    whole_batch = lax.all_gather(batch_rows, "tp", axis=0, tiled=True)
    inputs = jnp.take(whole_batch, chosen, axis=0)
    holders = holder_map[0]
    own_entry = jnp.take(holders, position)
    narrow = copies.shape[1]
    unit_cols = narrow // 8
    wide_cols = 7 * unit_cols
    scaling = 1.0 / math.sqrt(copies.shape[0])
    gate_pre = jnp.dot(inputs, copies, preferred_element_type=jnp.float32) * scaling
    logistic = jax.nn.sigmoid(gate_pre)
    gate_grad = (
        upstream.astype(jnp.float32)
        * up_act.astype(jnp.float32)
        * logistic
        * (1.0 + gate_pre * (1.0 - logistic))
    ).astype(jnp.bfloat16)
    tokens = gate_grad.shape[0]
    pooled = gathered_copies(gate_grad[:, wide_cols:], "tp", 1)
    pooled = pooled.reshape(tokens, tp_count, unit_cols)
    wanted = position * 7 + jnp.arange(7, dtype=jnp.int32)
    owners = jnp.argmax(holders[None, :] == wanted[:, None], axis=1)
    rebuilt = jnp.take(pooled, owners, axis=1).reshape(tokens, wide_cols)
    block_grad = jnp.where(own_entry == -2, rebuilt, gate_grad[:, :wide_cols])
    product = lax.dot_general(
        inputs, block_grad, (((0,), (0,)), ((), ())), preferred_element_type=jnp.float32
    )
    gradient = lax.psum_scatter(
        (product * scaling).astype(jnp.bfloat16), "rep", scatter_dimension=0, tiled=True
    ).astype(jnp.float32)
    first_new = beta_one * moment1.astype(jnp.float32) + (1.0 - beta_one) * gradient
    second_new = beta_two * moment2.astype(jnp.float32) + (1.0 - beta_two) * gradient * gradient
    step_size = first_new / bias_one / (jnp.sqrt(second_new / bias_two) + epsilon)
    master_next = master - learn_rate * (step_size + weight_decay * master)
    fresh_copy = master_next.astype(jnp.bfloat16)
    full_block = lax.all_gather(fresh_copy, "rep", axis=0, tiled=True)
    height = full_block.shape[0]
    failed_count = tp_count // 8
    root_list = jnp.nonzero(holders == -2, size=failed_count, fill_value=0)[0].astype(jnp.int32)
    slot_start = jnp.maximum(own_entry, 0) % 7 * unit_cols
    slot_ids = jnp.arange(failed_count, dtype=jnp.int32)
    my_slot = jnp.argmax(root_list == position)
    placing = (own_entry == -2) & (slot_ids == my_slot)
    placed = jnp.where(
        placing[None, :, None],
        full_block.astype(jnp.float32)[:, None, :],
        jnp.zeros((height, failed_count, wide_cols), jnp.float32),
    )
    summed = sum_in_two_steps(
        placed.reshape(height, failed_count * wide_cols).astype(jnp.bfloat16), "tp"
    ).astype(jnp.float32)
    summed = summed.astype(jnp.bfloat16)
    source_slot = jnp.argmax(root_list == jnp.maximum(own_entry, 0) // 7)
    adopted = lax.dynamic_slice_in_dim(summed, source_slot * wide_cols + slot_start, unit_cols, 1)
    adopted = jnp.where(own_entry >= 0, adopted, jnp.zeros_like(adopted))
    copy_next = jnp.concatenate([full_block, adopted], axis=1)
    copy_next = jnp.where(own_entry == -2, jnp.zeros_like(copy_next), copy_next)
    return (master_next, first_new.astype(jnp.bfloat16), second_new.astype(jnp.bfloat16), copy_next)


def solution(mesh):
    placed = (
        P(("rep", "tp"), None),
        P("rep", None),
        P("rep", None),
        P("rep", "tp"),
        P("rep", "tp"),
        P("rep", "tp"),
        P("rep", "tp"),
        P("rep", "tp"),
        P("rep", "tp"),
    )
    return jax.shard_map(
        on_device,
        mesh=mesh,
        in_specs=placed,
        out_specs=(P("rep", "tp"), P("rep", "tp"), P("rep", "tp"), P("rep", "tp")),
        check_vma=False,
    )
```

profile of v0, /device:TPU:0, one launch (start us, length us, event | category | flops | bytes accessed | tf_op | source)
XLA Modules:
  0.0 609.8 jit_solution(9419785542743542625)
XLA Ops:
  7.9 0.7 reduce.47
  8.6 0.7 fusion.9
  9.3 94.6 %all-gather.5.cloned.1.call-done = bf16[1536,4096]{1,0:T(8,128)(2,1)} async-done(((bf16[96,4096]{1,0:T(8,128)(2,1)}), bf16[1536,4096]{1,0:T(8,128)(2,1)}) %all-gather.5.cloned.1.call-update) | async-done | bytes 12582928 | tf_op jit(solution)/shard_map/all_gather | solution.py:55
  103.9 13.7 %gather_fusion = bf16[384,4096]{1,0:T(8,128)(2,1)S(1)} fusion(bf16[1536,4096]{1,0:T(8,128)(2,1)} %all-gather.5.cloned.1.call-done, s32[1024]{0:T(1024)S(1)} %pad_clamp_fusion.1), kind=kCustom, calls=%fused_computation | custom fusion | bytes 6292992 | tf_op jit(solution)/shard_map/jit(_take)/gather | solution.py:56
  117.6 8.9 %multiply_convert_fusion.1 = bf16[384,1024]{1,0:T(8,128)(2,1)S(1)} fusion(bf16[384,1024]{1,0:T(8,128)(2,1)} %param.14, bf16[384,1024]{1,0:T(8,128)(2,1)} %param.13, bf16[4096,1024]{1,0:T(8,128)(2,1)} %param.12, bf16[384,4096]{1,0:T(8,128)(2,1)S(1)} %gather_fusion, pred[384]{0:T(512)(128)(4,1)S(1)} %compare_and_fusion.2), kind=kOutput, calls=%fused_computation.12 | convolution fusion | flops 3227910144 | bytes 13894016 | tf_op jit(solution)/shard_map/dot_general | solution.py:63
  126.5 0.8 copy-done.3
  127.4 1.4 broadcast_in_dim.83
  128.8 3.8 all-to-all-start
  134.2 0.7 iota_reduce_fusion
  135.0 21.3 %all-to-all-done = bf16[16,384,128]{2,1,0:T(8,128)(2,1)S(1)} async-done(((bf16[16,384,128]{2,1,0:T(8,128)(2,1)}), bf16[16,384,128]{2,1,0:T(8,128)(2,1)S(1)}, u32[]{:S(2)}, u32[]{:S(2)}) %all-to-all-start) | async-done | bytes 1572896 | tf_op jit(solution)/shard_map/all_to_all | solution.py:19
  157.6 8.6 %multiply_convert_fusion = bf16[4096,896]{1,0:T(8,128)(2,1)} fusion(bf16[384,4096]{1,0:T(8,128)(2,1)} %copy-done, pred[384]{0:T(512)(128)(4,1)S(1)} %compare_and_fusion.2, bf16[384,1024]{1,0:T(8,128)(2,1)S(1)} %copy-done.4, bf16[384,896]{1,0:T(8,128)(2,1)S(1)} %copy.18, pred[896]{0:T(1024)(128)(4,1)S(1)} %broadcast_bitcast_fusion, pred[]{:T(512)} %bitcast.3), kind=kOutput, calls=%fused_computation.4 | convolution fusion | flops 2828173312 | bytes 11863553 | tf_op jit(solution)/shard_map/dot_general | solution.py:78
  166.3 81.2 %reduce-scatter.3.cloned.1.call-done = bf16[512,896]{1,0:T(8,128)(2,1)} async-done(((bf16[4096,896]{1,0:T(8,128)(2,1)}), bf16[512,896]{1,0:T(8,128)(2,1)}) %reduce-scatter.3.cloned.1.call-update) | async-done | bytes 917520 | tf_op jit(solution)/shard_map/reduce_scatter | solution.py:81
  247.5 5.7 fusion.17
  254.4 0.7 fusion.10
  255.1 1.4 compare_reduce_fusion.1
  257.2 77.0 %all-gather.7.cloned.1.call-done = bf16[4096,896]{1,0:T(8,128)(2,1)} async-done(((bf16[512,896]{1,0:T(8,128)(2,1)}), bf16[4096,896]{1,0:T(8,128)(2,1)}) %all-gather.7.cloned.1.call-update) | async-done | bytes 7340048 | tf_op jit(solution)/shard_map/all_gather | solution.py:89
  334.3 10.4 %broadcast_in_dim.91 = bf16[4096,2,896]{2,1,0:T(2,128)(2,1)} broadcast(bf16[4096,896]{1,0:T(8,128)(2,1)} %all-gather.7.cloned.1.call-done), dimensions={0,2} | broadcast | bytes 22020096 | tf_op jit(solution)/shard_map/jit(_where)/broadcast_in_dim | solution.py:97
  344.7 10.0 %copy.20 = bf16[512,8,2,896]{3,1,2,0:T(8,128)(2,1)S(1)} copy(bf16[512,8,2,896]{3,2,1,0:T(2,128)(2,1)} %bitcast.29) | data formatting | bytes 29360128
  354.7 7.2 %select_convert_fusion = bf16[4096,1792]{1,0:T(8,128)(2,1)} fusion(bf16[4096,1792]{1,0:T(8,128)(2,1)S(1)} %bitcast.28, pred[1792]{0:T(1024)(128)(4,1)S(1)} %broadcast_in_dim.89), kind=kLoop, calls=%fused_computation.3 | loop fusion | flops 7340032 | bytes 29361920 | tf_op jit(solution)/shard_map/convert_element_type | solution.py:103
  362.0 131.4 %reduce-scatter.5.cloned.1.call-done = bf16[256,1792]{1,0:T(8,128)(2,1)} async-done(((bf16[4096,1792]{1,0:T(8,128)(2,1)}), bf16[256,1792]{1,0:T(8,128)(2,1)}) %reduce-scatter.5.cloned.1.call-update) | async-done | bytes 917520 | tf_op jit(solution)/shard_map/reduce_scatter | solution.py:42
  493.5 1.3 compare_reduce_fusion
  495.4 99.1 %all-gather.9.cloned.1.call-done = bf16[4096,1792]{1,0:T(8,128)(2,1)} async-done(((bf16[256,1792]{1,0:T(8,128)(2,1)}), bf16[4096,1792]{1,0:T(8,128)(2,1)}) %all-gather.9.cloned.1.call-update) | async-done | bytes 14680080 | tf_op jit(solution)/shard_map/all_gather | solution.py:45
  594.5 1.4 dynamic-slice_select_fusion
  596.0 7.3 %maximum_select_fusion = bf16[4096,1024]{1,0:T(8,128)(2,1)} fusion(bf16[4096,128]{1,0:T(8,128)(2,1)S(1)} %dynamic-slice_select_fusion, bf16[4096,896]{1,0:T(8,128)(2,1)} %all-gather.7.cloned.1.call-done, pred[]{:T(512)} %bitcast.3), kind=kLoop, calls=%fused_computation.5 | loop fusion | flops 20971520 | bytes 16777216 | tf_op jit(solution)/shard_map/jit(_where)/select_n | solution.py:110
  (43 shorter events, 5.1 us)
Async XLA Ops:
  7.2 96.7 %all-gather.5.cloned.1.call-start = ((), (), s32[]{:S(2)}) async-start(), calls=%async_computation.3 | async-start | bytes 13369344 | tf_op jit(solution)/shard_map/all_gather | solution.py:55
  117.6 8.9 %copy-start = (bf16[384,4096]{1,0:T(8,128)(2,1)}, bf16[384,4096]{1,0:T(8,128)(2,1)S(1)}, u32[]{:S(2)}) copy-start(bf16[384,4096]{1,0:T(8,128)(2,1)S(1)} %gather_fusion) | copy-start | bytes 9437188
  126.5 0.9 copy-start.3
  128.8 4.1 copy-start.5
  128.8 27.4 %all-to-all-start = ((bf16[16,384,128]{2,1,0:T(8,128)(2,1)}), bf16[16,384,128]{2,1,0:T(8,128)(2,1)S(1)}, u32[]{:S(2)}, u32[]{:S(2)}) async-start(bf16[16,384,128]{2,1,0:T(8,128)(2,1)} %broadcast_in_dim.83), calls=%async_computation | async-start | bytes 3145728 | tf_op jit(solution)/shard_map/all_to_all | solution.py:19
  132.7 114.8 %reduce-scatter.3.cloned.1.call-start = ((), (), s32[]{:S(2)}) async-start(), calls=%async_computation.4 | async-start | bytes 8257536 | tf_op jit(solution)/shard_map/reduce_scatter | solution.py:81
  156.2 1.4 copy-start.4
  166.2 81.2 %copy-start.1 = (f32[512,896]{1,0:T(8,128)S(1)}, f32[512,896]{1,0:T(8,128)}, u32[]{:S(2)}) copy-start(f32[512,896]{1,0:T(8,128)} %param.15) | copy-start | bytes 5505028
  166.2 81.2 %copy-start.2 = (bf16[512,896]{1,0:T(8,128)(2,1)S(1)}, bf16[512,896]{1,0:T(8,128)(2,1)}, u32[]{:S(2)}) copy-start(bf16[512,896]{1,0:T(8,128)(2,1)} %param.17) | copy-start | bytes 2752516
  166.3 168.0 %all-gather.7.cloned.1.call-start = ((), (), s32[]{:S(2)}) async-start(), calls=%async_computation.5 | async-start | bytes 8257536 | tf_op jit(solution)/shard_map/all_gather | solution.py:89
  253.2 240.2 %reduce-scatter.5.cloned.1.call-start = ((), (), s32[]{:S(2)}) async-start(), calls=%async_computation.6 | async-start | bytes 15597568 | tf_op jit(solution)/shard_map/reduce_scatter | solution.py:42
  362.0 232.5 %all-gather.9.cloned.1.call-start = ((), (), s32[]{:S(2)}) async-start(), calls=%async_computation.7 | async-start | bytes 15597568 | tf_op jit(solution)/shard_map/all_gather | solution.py:45
Sparse Core Ops, SparseCore 0:
  10.4 93.4 all-gather.4
  166.4 81.0 reduce-scatter.2
  253.3 80.8 all-gather.6
  362.1 131.2 reduce-scatter.4
  496.0 98.4 all-gather.8
where the time goes:
time: 612 us; the launch traced here: 610 us
  waiting for transfers between devices  505 us (83%)
  local copies, waits for them, and re-layouts  38.7 us (6%)
  other arithmetic  29 us (5%)
  matrix products  17.5 us (3%)
  between operations  15.2 us (2%)
    reduce_scatter x1, waiting for transfers between devices, sum_in_two_steps(): lax.psum_scatter(rows_for(lines, lax.axis_size(axis)), axis, scatter_dime...  131 us
    all_gather x1, waiting for transfers between devices, sum_in_two_steps(): whole = lax.all_gather(own, axis).reshape(-1, *lines.shape[1:])  99.1 us
    all_gather x1, waiting for transfers between devices, on_device(): whole_batch = lax.all_gather(batch_rows, 'tp', axis=0, tiled=True)  94.6 us
    reduce_scatter x1, waiting for transfers between devices, on_device(): lax.psum_scatter((product * scaling).astype(jnp.bfloat16), 'rep', scatter...  81.2 us
    all_gather x1, waiting for transfers between devices, on_device(): full_block = lax.all_gather(fresh_copy, 'rep', axis=0, tiled=True)  77 us
    all_to_all x1, waiting for transfers between devices, from_everyone(): return lax.all_to_all(copies, axis, split_axis=0, concat_axis=0, tiled=True)  21.3 us
    gather x1, local copies, waits for them, and re-layouts, on_device(): inputs = jnp.take(whole_batch, chosen, axis=0)  13.7 us
  transfers between devices with their start and end apart: 6, of which 6 were waited for; matrix products, arithmetic and copies ran while one was open for 1% of the time, Pallas kernels for 0%

commit v1 on v0

v1 whole, which is shorter than its diff:
```python
import math

import jax
import jax.numpy as jnp
from jax import lax
from jax.sharding import PartitionSpec as P

beta_one = 0.9
beta_two = 0.95
bias_one = 1.0 - 0.9**10
bias_two = 1.0 - 0.95**10
learn_rate = 0.05
weight_decay = 0.1
epsilon = 1e-08


def picked(indices, table):
    one_hot = (indices[:, None] == jnp.arange(table.shape[0], dtype=jnp.int32)[None, :]).astype(jnp.bfloat16)
    return jnp.dot(one_hot, table, preferred_element_type=jnp.float32).astype(jnp.bfloat16)


def on_device(
    batch_rows, token_slots, holder_map, copies, upstream, up_act, master, moment1, moment2
):
    tp_count = lax.axis_size("tp")
    rep_count = lax.axis_size("rep")
    position = lax.axis_index("tp")
    holders = holder_map[0]
    own_entry = jnp.sum(jnp.where(jnp.arange(tp_count) == position, holders, 0))
    all_holders = lax.all_gather(holders, "rep")
    unit_cols = copies.shape[1] // 8
    wide_cols = 7 * unit_cols
    scaling = 1.0 / math.sqrt(copies.shape[0])

    columns = lax.all_to_all(batch_rows, "tp", split_axis=1, concat_axis=0, tiled=True)
    chosen = picked(token_slots[0], columns)
    inputs = lax.all_gather(chosen, "tp", axis=1, tiled=True)
    gate_pre = jnp.dot(inputs, copies, preferred_element_type=jnp.float32) * scaling
    logistic = jax.nn.sigmoid(gate_pre)
    gate_grad = (
        upstream.astype(jnp.float32)
        * up_act.astype(jnp.float32)
        * logistic
        * (1.0 + gate_pre * (1.0 - logistic))
    ).astype(jnp.bfloat16)
    tokens = gate_grad.shape[0]
    pooled = lax.all_to_all(
        jnp.broadcast_to(gate_grad[:, wide_cols:], (tp_count, tokens, unit_cols)),
        "tp", split_axis=0, concat_axis=0, tiled=True,
    )
    wanted = position * 7 + jnp.arange(7, dtype=jnp.int32)
    choice = (holders[None, :] == wanted[:, None]).astype(jnp.bfloat16)
    rebuilt = jnp.concatenate(
        [
            jnp.sum(jnp.where(choice[s, :, None, None] > 0, pooled, jnp.zeros_like(pooled)), axis=0)
            for s in range(7)
        ],
        axis=1,
    )
    block_grad = jnp.where(own_entry == -2, rebuilt, gate_grad[:, :wide_cols])
    product = lax.dot_general(
        inputs, block_grad, (((0,), (0,)), ((), ())), preferred_element_type=jnp.float32
    )
    gradient = lax.psum_scatter(
        (product * scaling).astype(jnp.bfloat16), "rep", scatter_dimension=0, tiled=True
    ).astype(jnp.float32)
    first_new = beta_one * moment1.astype(jnp.float32) + (1.0 - beta_one) * gradient
    second_new = beta_two * moment2.astype(jnp.float32) + (1.0 - beta_two) * gradient * gradient
    step_size = first_new / bias_one / (jnp.sqrt(second_new / bias_two) + epsilon)
    master_next = master - learn_rate * (step_size + weight_decay * master)
    fresh = master_next.astype(jnp.bfloat16)
    full_block = lax.all_gather(fresh, "rep", axis=0, tiled=True)

    own_rows = fresh.shape[0]
    strip = own_rows // tp_count
    spread = lax.all_to_all(fresh, "tp", split_axis=0, concat_axis=0, tiled=True)
    table = spread.reshape(tp_count, strip, 7, unit_cols).transpose(0, 2, 1, 3)
    routed = picked(all_holders.reshape(-1), table.reshape(tp_count * 7, strip * unit_cols))
    routed = routed.reshape(rep_count, tp_count, strip, unit_cols)
    routed = lax.all_to_all(routed, "tp", split_axis=1, concat_axis=2, tiled=True)
    routed = routed.reshape(rep_count * own_rows, unit_cols)
    adopted = lax.all_to_all(routed, "rep", split_axis=0, concat_axis=0, tiled=True)
    copy_next = jnp.concatenate([full_block, adopted], axis=1)
    copy_next = jnp.where(own_entry == -2, jnp.zeros_like(copy_next), copy_next)
    return (master_next, first_new.astype(jnp.bfloat16), second_new.astype(jnp.bfloat16), copy_next)


def solution(mesh):
    placed = (
        P(("rep", "tp"), None),
        P("rep", None),
        P("rep", None),
        P("rep", "tp"),
        P("rep", "tp"),
        P("rep", "tp"),
        P("rep", "tp"),
        P("rep", "tp"),
        P("rep", "tp"),
    )
    return jax.shard_map(
        on_device,
        mesh=mesh,
        in_specs=placed,
        out_specs=(P("rep", "tp"), P("rep", "tp"), P("rep", "tp"), P("rep", "tp")),
        check_vma=False,
    )
```

time: 612 us -> 367 us (0.60)
  waiting for transfers between devices: 505 us -> 232 us
  blocking collectives: 0 us -> 61.1 us
  local copies, waits for them, and re-layouts: 38.7 us -> 6.07 us
  starting transfers between devices: 4.23 us -> 18.8 us
  other arithmetic: 29 us -> 17.5 us
    all_gather x3 -> x2, waiting for transfers between devices: 271 us -> 51.7 us  [the longest x1 51.7 us: on_device(): inputs = lax.all_gather(chosen, 'tp', axis=1, tiled=True)]
    reduce_scatter x1 -> x0, waiting for transfers between devices: 131 us -> none  [sum_in_two_steps(): lax.psum_scatter(rows_for(lines, lax.axis_size(axis)), axis, scatter_dime...]
    all_to_all x1 -> x3, waiting for transfers between devices: 21.3 us -> 98 us  [the longest x1 60.8 us: on_device(): lax.all_to_all(fresh, 'tp', split_axis=0, concat_axis=0, tiled=True)]
    all_to_all x0 -> x2, blocking collectives: none -> 40.4 us  [the longest x1 22.6 us: on_device(): lax.all_to_all(routed, 'tp', split_axis=1, concat_axis=2, tiled=True)]
    all_gather x0 -> x1, blocking collectives: none -> 20.7 us  [on_device(): all_holders = lax.all_gather(holders, 'rep')]
    gather x4 -> x0, local copies, waits for them, and re-layouts: 15.1 us -> none  [the longest x1 13.7 us: on_device(): inputs = jnp.take(whole_batch, chosen, axis=0)]
    all_to_all x1 -> x3, starting transfers between devices: 3.84 us -> 18.7 us  [the longest x1 8.1 us: on_device(): lax.all_to_all(batch_rows, 'tp', split_axis=1, concat_axis=0, tiled=True)]
    broadcast_in_dim x5 -> x1, local copies, waits for them, and re-layouts: 12.1 us -> 1.45 us  [on_device(): jnp.broadcast_to(gate_grad[:, wide_cols:], (tp_count, tokens, unit_cols))]
  transfers between devices with their start and end apart: 6 -> 6, of which waited for: 6 -> 5; matrix products, arithmetic and copies ran while one was open for 1% -> 1% of each run, Pallas kernels for 0% -> 0%
where the time goes in v1:
time: 367 us; the launch traced here: 366 us
  waiting for transfers between devices  232 us (63%)
  blocking collectives  61.1 us (17%)
  starting transfers between devices  18.8 us (5%)
  other arithmetic  17.5 us (5%)
  matrix products  16.4 us (4%)
  between operations  14.6 us (4%)
  local copies, waits for them, and re-layouts  6.07 us (2%)
    reduce_scatter x1, waiting for transfers between devices, on_device(): lax.psum_scatter((product * scaling).astype(jnp.bfloat16), 'rep', scatter...  81.7 us
    all_to_all x1, waiting for transfers between devices, on_device(): lax.all_to_all(fresh, 'tp', split_axis=0, concat_axis=0, tiled=True)  60.8 us
    all_gather x1, waiting for transfers between devices, on_device(): inputs = lax.all_gather(chosen, 'tp', axis=1, tiled=True)  51.7 us
    all_to_all x1, blocking collectives, on_device(): lax.all_to_all(routed, 'tp', split_axis=1, concat_axis=2, tiled=True)  22.6 us
    all_to_all x1, waiting for transfers between devices, on_device(): lax.all_to_all(jnp.broadcast_to(gate_grad[:, wide_cols:], (tp_count, toke...  22.1 us
    all_gather x1, blocking collectives, on_device(): all_holders = lax.all_gather(holders, 'rep')  20.7 us
    all_to_all x1, blocking collectives, on_device(): lax.all_to_all(routed, 'rep', split_axis=0, concat_axis=0, tiled=True)  17.8 us
    all_to_all x1, waiting for transfers between devices, on_device(): lax.all_to_all(batch_rows, 'tp', split_axis=1, concat_axis=0, tiled=True)  15.1 us
  transfers between devices with their start and end apart: 6, of which 5 were waited for; matrix products, arithmetic and copies ran while one was open for 1% of the time, Pallas kernels for 0%

profile of v1, /device:TPU:0, one launch (start us, length us, event | category | flops | bytes accessed | tf_op | source)
XLA Modules:
  0.0 366.0 jit_solution(13121369228132547831)
XLA Ops:
  7.2 2.1 copy.35
  9.3 8.1 %all-to-all-start = ((bf16[96,16,256]{2,0,1:T(8,128)(2,1)}), bf16[96,16,256]{2,0,1:T(8,128)(2,1)S(1)}, u32[]{:S(2)}, u32[]{:S(2)}) async-start(bf16[96,16,256]{2,0,1:T(8,128)(2,1)} %bitcast.40), calls=%async_computation | async-start | bytes 1572864 | tf_op jit(solution)/shard_map/all_to_all | solution.py:35
  17.5 15.1 %all-to-all-done = bf16[96,16,256]{2,0,1:T(8,128)(2,1)S(1)} async-done(((bf16[96,16,256]{2,0,1:T(8,128)(2,1)}), bf16[96,16,256]{2,0,1:T(8,128)(2,1)S(1)}, u32[]{:S(2)}, u32[]{:S(2)}) %all-to-all-start) | async-done | bytes 786464 | tf_op jit(solution)/shard_map/all_to_all | solution.py:35
  32.6 1.2 fusion.7
  33.8 51.7 %all-gather.4.cloned.1.call-done = bf16[384,4096]{1,0:T(8,128)(2,1)} async-done(((bf16[384,256]{1,0:T(8,128)(2,1)}), bf16[384,4096]{1,0:T(8,128)(2,1)}) %all-gather.4.cloned.1.call-update) | async-done | bytes 3145744 | tf_op jit(solution)/shard_map/all_gather | solution.py:37
  85.6 8.3 %multiply_convert_fusion.1 = bf16[384,1024]{1,0:T(8,128)(2,1)S(1)} fusion(bf16[384,1024]{1,0:T(8,128)(2,1)S(1)} %copy-done.5, bf16[384,1024]{1,0:T(8,128)(2,1)S(1)} %copy-done.6, bf16[384,4096]{1,0:T(8,128)(2,1)} %all-gather.4.cloned.1.call-done, bf16[4096,1024]{1,0:T(8,128)(2,1)} %param.12), kind=kOutput, calls=%fused_computation.17 | convolution fusion | flops 3226337280 | bytes 13893632 | tf_op jit(solution)/shard_map/dot_general | solution.py:38
  93.9 1.4 broadcast_in_dim.53
  95.3 3.9 %all-to-all-start.1 = ((bf16[16,384,128]{2,1,0:T(8,128)(2,1)}), bf16[16,384,128]{2,1,0:T(8,128)(2,1)S(1)}, u32[]{:S(2)}, u32[]{:S(2)}) async-start(bf16[16,384,128]{2,1,0:T(8,128)(2,1)} %broadcast_in_dim.53), calls=%async_computation.1 | async-start | bytes 3145728 | tf_op jit(solution)/shard_map/all_to_all | solution.py:47
  99.3 0.6 fusion.12
  100.6 22.1 %all-to-all-done.1 = bf16[16,384,128]{2,1,0:T(8,128)(2,1)S(1)} async-done(((bf16[16,384,128]{2,1,0:T(8,128)(2,1)}), bf16[16,384,128]{2,1,0:T(8,128)(2,1)S(1)}, u32[]{:S(2)}, u32[]{:S(2)}) %all-to-all-start.1) | async-done | bytes 1572896 | tf_op jit(solution)/shard_map/all_to_all | solution.py:47
  122.8 3.0 select_reduce_fusion
  126.0 6.4 %multiply_convert_fusion = bf16[4096,896]{1,0:T(8,128)(2,1)} fusion(bf16[384,4096]{1,0:T(8,128)(2,1)S(1)} %copy-done.4, bf16[384,896]{1,0:T(8,128)(2,1)S(1)} %constant_dynamic-update-slice_fusion, bf16[384,1024]{1,0:T(8,128)(2,1)S(1)} %multiply_convert_fusion.1, pred[]{:T(512)S(6)} %eq.59), kind=kOutput, calls=%fused_computation | convolution fusion | flops 2826256384 | bytes 11862017 | tf_op jit(solution)/shard_map/dot_general | solution.py:61
  132.5 81.7 %reduce-scatter.2.cloned.1.call-done = bf16[512,896]{1,0:T(8,128)(2,1)} async-done(((bf16[4096,896]{1,0:T(8,128)(2,1)}), bf16[512,896]{1,0:T(8,128)(2,1)}) %reduce-scatter.2.cloned.1.call-update) | async-done | bytes 917520 | tf_op jit(solution)/shard_map/reduce_scatter | solution.py:64
  214.3 5.7 %fusion.13 = (bf16[512,896]{1,0:T(8,128)(2,1)}, f32[512,896]{1,0:T(8,128)}, bf16[512,896]{1,0:T(8,128)(2,1)}, bf16[512,896]{1,0:T(8,128)(2,1)}) fusion(f32[512,896]{1,0:T(8,128)S(1)} %copy-done, bf16[512,896]{1,0:T(8,128)(2,1)S(1)} %copy-done.1, bf16[512,896]{1,0:T(8,128)(2,1)} %reduce-scatter.2.cloned.1.call-done, bf16[512,896]{1,0:T(8,128)(2,1)} %param.16), kind=kLoop, calls=%fused_computation.48 | loop fusion | flops 9633792 | bytes 9175040 | tf_op jit(solution)/shard_map/convert_element_type | solution.py:71
  220.0 6.7 %all-to-all-start.2 = ((bf16[16,32,896]{2,1,0:T(8,128)(2,1)}), bf16[16,32,896]{2,1,0:T(8,128)(2,1)S(1)}, u32[]{:S(2)}, u32[]{:S(2)}) async-start(bf16[16,32,896]{2,1,0:T(8,128)(2,1)} %bitcast.41), calls=%async_computation.3 | async-start | bytes 1835008 | tf_op jit(solution)/shard_map/all_to_all | solution.py:76
  226.7 20.7 %all-gather = s32[8,1,16]{2,1,0:T(1,128)S(1)} all-gather(s32[1,1,16]{2,1,0:T(1,128)S(1)} %bitcast.50), channel_id=1, replica_groups=mesh['rep'=8,'tp'=16] {'rep'}, dimensions={0}, use_global_device_ids=true | all-gather | bytes 576 | tf_op jit(solution)/shard_map/all_gather | solution.py:30
  247.4 0.6 broadcast.92
  248.0 0.7 reduce.11
  248.8 60.8 %all-to-all-done.2 = bf16[16,32,896]{2,1,0:T(8,128)(2,1)S(1)} async-done(((bf16[16,32,896]{2,1,0:T(8,128)(2,1)}), bf16[16,32,896]{2,1,0:T(8,128)(2,1)S(1)}, u32[]{:S(2)}, u32[]{:S(2)}) %all-to-all-start.2) | async-done | bytes 917536 | tf_op jit(solution)/shard_map/all_to_all | solution.py:76
  309.6 1.0 reshape.100
  310.8 0.5 fusion.5
  311.7 22.6 %all_to_all.54 = bf16[8,16,32,128]{3,2,0,1:T(8,128)(2,1)S(1)} all-to-all(bf16[8,16,32,128]{3,2,0,1:T(8,128)(2,1)S(1)} %copy.25), channel_id=1, replica_groups=mesh['rep'=8,'tp'=16] {'tp'}, dimensions={1} | all-to-all | bytes 2097152 | tf_op jit(solution)/shard_map/all_to_all | solution.py:80
  334.4 17.8 %all_to_all.55 = bf16[8,512,128]{2,1,0:T(8,128)(2,1)S(1)} all-to-all(bf16[8,512,128]{2,1,0:T(8,128)(2,1)S(1)} %bitcast.44), channel_id=1, replica_groups=mesh['rep'=8,'tp'=16] {'rep'}, dimensions={0} | all-to-all | bytes 2097152 | tf_op jit(solution)/shard_map/all_to_all | solution.py:82
  352.1 7.3 %maximum_select_fusion = bf16[4096,1024]{1,0:T(8,128)(2,1)} fusion(bf16[4096,128]{1,0:T(8,128)(2,1)S(1)} %bitcast.42, bf16[4096,896]{1,0:T(8,128)(2,1)} %all-gather.6.cloned.1.call-done, pred[]{:T(512)S(6)} %eq.59), kind=kLoop, calls=%fused_computation.1 | loop fusion | flops 20971520 | bytes 16777216 | tf_op jit(solution)/shard_map/jit(_where)/select_n | solution.py:84
  (38 shorter events, 1.2 us)
Async XLA Ops:
  7.2 10.3 %copy-start.3 = (s32[1,384]{1,0:T(1,128)S(1)}, s32[1,384]{1,0:T(1,128)}, u32[]{:S(2)}) copy-start(s32[1,384]{1,0:T(1,128)} %param.10) | copy-start | bytes 4612
  9.3 76.3 %copy-start.5 = (bf16[384,1024]{1,0:T(8,128)(2,1)S(1)}, bf16[384,1024]{1,0:T(8,128)(2,1)}, u32[]{:S(2)}) copy-start(bf16[384,1024]{1,0:T(8,128)(2,1)} %param.14) | copy-start | bytes 2359300
  9.3 76.3 %copy-start.6 = (bf16[384,1024]{1,0:T(8,128)(2,1)S(1)}, bf16[384,1024]{1,0:T(8,128)(2,1)}, u32[]{:S(2)}) copy-start(bf16[384,1024]{1,0:T(8,128)(2,1)} %param.13) | copy-start | bytes 2359300
  9.3 23.3 %all-to-all-start = ((bf16[96,16,256]{2,0,1:T(8,128)(2,1)}), bf16[96,16,256]{2,0,1:T(8,128)(2,1)S(1)}, u32[]{:S(2)}, u32[]{:S(2)}) async-start(bf16[96,16,256]{2,0,1:T(8,128)(2,1)} %bitcast.40), calls=%async_computation | async-start | bytes 1572864 | tf_op jit(solution)/shard_map/all_to_all | solution.py:35
  17.4 68.2 %all-gather.4.cloned.1.call-start = ((), (), s32[]{:S(2)}) async-start(), calls=%async_computation.6 | async-start | bytes 3342336 | tf_op jit(solution)/shard_map/all_gather | solution.py:37
  95.3 3.9 %copy-start.2 = (s32[1,16]{1,0:T(1,128)S(1)}, s32[1,16]{1,0:T(1,128)}, u32[]{:S(2)}) copy-start(s32[1,16]{1,0:T(1,128)} %param.11) | copy-start | bytes 196
  95.3 27.5 %all-to-all-start.1 = ((bf16[16,384,128]{2,1,0:T(8,128)(2,1)}), bf16[16,384,128]{2,1,0:T(8,128)(2,1)S(1)}, u32[]{:S(2)}, u32[]{:S(2)}) async-start(bf16[16,384,128]{2,1,0:T(8,128)(2,1)} %broadcast_in_dim.53), calls=%async_computation.1 | async-start | bytes 3145728 | tf_op jit(solution)/shard_map/all_to_all | solution.py:47
  99.2 115.1 %reduce-scatter.2.cloned.1.call-start = ((), (), s32[]{:S(2)}) async-start(), calls=%async_computation.7 | async-start | bytes 8257536 | tf_op jit(solution)/shard_map/reduce_scatter | solution.py:64
  122.8 3.2 copy-start.4
  132.4 81.8 %copy-start = (f32[512,896]{1,0:T(8,128)S(1)}, f32[512,896]{1,0:T(8,128)}, u32[]{:S(2)}) copy-start(f32[512,896]{1,0:T(8,128)} %param.15) | copy-start | bytes 5505028
  132.4 81.8 %copy-start.1 = (bf16[512,896]{1,0:T(8,128)(2,1)S(1)}, bf16[512,896]{1,0:T(8,128)(2,1)}, u32[]{:S(2)}) copy-start(bf16[512,896]{1,0:T(8,128)(2,1)} %param.17) | copy-start | bytes 2752516
  132.5 219.7 %all-gather.6.cloned.1.call-start = ((), (), s32[]{:S(2)}) async-start(), calls=%async_computation.8 | async-start | bytes 8257536 | tf_op jit(solution)/shard_map/all_gather | solution.py:72
  220.0 89.6 %all-to-all-start.2 = ((bf16[16,32,896]{2,1,0:T(8,128)(2,1)}), bf16[16,32,896]{2,1,0:T(8,128)(2,1)S(1)}, u32[]{:S(2)}, u32[]{:S(2)}) async-start(bf16[16,32,896]{2,1,0:T(8,128)(2,1)} %bitcast.41), calls=%async_computation.3 | async-start | bytes 1835008 | tf_op jit(solution)/shard_map/all_to_all | solution.py:76
Sparse Core Ops, SparseCore 0:
  33.9 51.5 all-gather.3
  132.6 81.6 reduce-scatter.1
  220.1 88.2 all-gather.5

commit v2 on v1

v2 whole, which is shorter than its diff:
```python
import functools
import math

import jax
import jax.numpy as jnp
from jax import lax
from jax.experimental import pallas as pl
from jax.experimental.pallas import tpu as pltpu
from jax.sharding import PartitionSpec as P

beta_one = 0.9
beta_two = 0.95
bias_one = 1.0 - 0.9**10
bias_two = 1.0 - 0.95**10
learn_rate = 0.05
weight_decay = 0.1
epsilon = 1e-08

D, TOK, WIDE, UNIT, NARROW = 4096, 384, 896, 128, 1024
REP, TP = 8, 16
OWN, SHARE = 96, 256
ROWS = D // REP
STRIP = ROWS // TP
SEVEN = WIDE // UNIT
PART = TOK // (TP // 2)
SCALING = 1.0 / math.sqrt(D)
MESH = pl.DeviceIdType.MESH
F32, BF16 = jnp.float32, jnp.bfloat16


class Place:
    def __init__(self):
        r, t = lax.axis_index("rep"), lax.axis_index("tp")
        self.r, self.t = r, t
        x, zl = r % 4, r // 4
        y, zh, c = t // 4, (t // 2) % 2, t % 2
        self.core = c
        self.chip = t // 2
        self.sibling = (r, t + 1 - 2 * c)

        def rep_id(step, flip):
            return (x + step) % 4 + 4 * ((zl + flip) % 2)

        def tp_id(step, flip):
            return ((y + step) % 4) * 4 + ((zh + flip) % 2) * 2 + c

        self.rep_ids = [[rep_id(s, f) for s in (0, 1, 3, 2)] for f in (0, 1)]
        self.tp_ids = [[tp_id(s, f) for s in (0, 1, 3, 2)] for f in (0, 1)]

    def rep_dev(self, other):
        return (other, self.t)

    def tp_dev(self, other):
        return (self.r, other)


def greet(place):
    barrier = pltpu.get_barrier_semaphore()

    def rep_mate(k, carry):
        pl.semaphore_signal(barrier, inc=1, device_id=((place.r + k) % REP, place.t), device_id_type=MESH)
        return carry

    def tp_mate(k, carry):
        pl.semaphore_signal(barrier, inc=1, device_id=(place.r, (place.t + k) % TP), device_id_type=MESH)
        return carry

    lax.fori_loop(1, REP, rep_mate, 0)
    lax.fori_loop(1, TP, tp_mate, 0)
    pl.semaphore_wait(barrier, REP + TP - 2)


class Tree:
    def __init__(self, view, ids, dev, ssem, rsem, extent, first):
        (me, nx, pv, op), (me_p, nx_p, pv_p, op_p) = ids
        to_nx, to_pv, to_pair = dev(nx), dev(pv), dev(me_p)
        half, a_half, rest = extent // 2, first // 2, extent - first
        self.rest, self.names = rest, dict(me=me, nx=nx, pv=pv, op=op, me_p=me_p, nx_p=nx_p, pv_p=pv_p, op_p=op_p)
        sent = {
            1: (me, 0, extent, to_nx), 2: (me, 0, extent, to_pv), 3: (me, 0, first, to_pair), 4: (me, first, rest, to_pair),
            5: (me_p, 0, first, to_nx), 6: (me_p, 0, first, to_pv), 7: (pv, 0, half, to_nx), 8: (nx, half, half, to_pv),
            9: (pv_p, 0, a_half, to_nx), 10: (nx_p, a_half, a_half, to_pv),
            11: (pv, first, rest, to_pair), 12: (nx, first, rest, to_pair), 13: (op, first, rest, to_pair),
        }
        got = {1: pv, 2: nx, 3: me_p, 4: me_p, 5: pv_p, 6: nx_p, 7: op, 8: op, 9: op_p, 10: op_p, 11: pv_p, 12: nx_p, 13: op_p}
        skipped = () if rest else (4, 11, 12, 13)
        self.out, self.into = {}, {}
        for i, (chunk, low, count, to) in sent.items():
            if i not in skipped:
                for book, which in ((self.out, chunk), (self.into, got[i])):
                    ref = view(which, low, count)
                    book[i] = pltpu.make_async_remote_copy(
                        src_ref=ref, dst_ref=ref, send_sem=ssem.at[i - 1], recv_sem=rsem.at[i - 1],
                        device_id=to, device_id_type=MESH,
                    )

    def start(self, *which):
        for i in which:
            if i in self.out:
                self.out[i].start()

    def wait(self, *which):
        for i in which:
            if i in self.into:
                self.into[i].wait_recv()

    def steps(self, done):
        def pair():
            self.wait(3)
            self.start(5, 6)
            if not self.rest:
                done("me_p")

        def previous():
            self.wait(1)
            self.start(7, 11)
            done("pv")

        def following():
            self.wait(2)
            self.start(8, 12)
            done("nx")

        def pair_previous():
            self.wait(5)
            self.start(9)
            if not self.rest:
                done("pv_p")

        def pair_following():
            self.wait(6)
            self.start(10)
            if not self.rest:
                done("nx_p")

        def opposite():
            self.wait(7, 8)
            self.start(13)
            done("op")

        def rests():
            if self.rest:
                self.wait(4)
                done("me_p")
                self.wait(11)
                done("pv_p")
                self.wait(12)
                done("nx_p")

        def last():
            self.wait(9, 10, 13)
            done("op_p")

        return [pair, previous, following, pair_previous, pair_following, opposite, rests, last]

    def begin(self):
        self.start(3, 1, 2, 4)

    def drain(self):
        for copy in self.out.values():
            copy.wait_send()


ORDER = ("me", "pv", "nx", "me_p", "op", "pv_p", "nx_p", "op_p")


class Siblings:
    def __init__(self, tree, view, extent, place, ssem, rsem):
        self.out, self.into = {}, {}
        for n, name in enumerate(ORDER):
            mine = tree.names[name]
            for book, which in ((self.out, mine), (self.into, mine + 1 - 2 * place.core)):
                ref = view(which, 0, extent)
                book[name] = pltpu.make_async_remote_copy(
                    src_ref=ref, dst_ref=ref, send_sem=ssem.at[n], recv_sem=rsem.at[n],
                    device_id=place.sibling, device_id_type=MESH,
                )

    def start(self, name):
        self.out[name].start()

    def wait(self, name):
        self.into[name].wait_recv()

    def drain(self):
        for copy in self.out.values():
            copy.wait_send()


def front_kernel(
    rows_ref, slots_ref, holders_ref, map_ref, copies_ref, upstream_ref, act_ref,
    inputs_out, grad_out, holders_out,
    own_rows, spread, inputs, weight, total, grad, pieces,
    map_s, map_r, row_s, row_r, tree_s, tree_r, sib_s, sib_r, tree2_s, tree2_r, sib2_s, sib2_r, local,
):
    place = Place()
    t = place.t
    load_rows = pltpu.make_async_copy(rows_ref, own_rows, local.at[0])
    load_rows.start()
    load_weight = pltpu.make_async_copy(copies_ref, weight, local.at[1])
    load_weight.start()
    greet(place)
    load_rows.wait()

    def share_to(k):
        to = (t + k) % TP
        return pltpu.make_async_remote_copy(
            src_ref=own_rows.at[:, pl.ds(pl.multiple_of(to * SHARE, SHARE), SHARE)],
            dst_ref=spread.at[pl.ds(pl.multiple_of(t * OWN, OWN), OWN), :],
            send_sem=row_s.at[k], recv_sem=row_r.at[k],
            device_id=(place.r, to), device_id_type=MESH,
        )

    def share_from(k):
        source = (t + TP - k) % TP
        ref = spread.at[pl.ds(pl.multiple_of(source * OWN, OWN), OWN), :]
        return pltpu.make_async_remote_copy(
            src_ref=ref, dst_ref=ref, send_sem=row_s.at[k], recv_sem=row_r.at[k],
            device_id=(place.r, source), device_id_type=MESH,
        )

    lax.fori_loop(1, TP, lambda k, c: (share_to(k).start(), c)[1], 0)

    def map_to(k):
        return pltpu.make_async_remote_copy(
            src_ref=map_ref, dst_ref=holders_out.at[place.r], send_sem=map_s.at[k], recv_sem=map_r.at[k],
            device_id=((place.r + k) % REP, t), device_id_type=MESH,
        )

    def map_from(k):
        source = (place.r + REP - k) % REP
        return pltpu.make_async_remote_copy(
            src_ref=map_ref, dst_ref=holders_out.at[source], send_sem=map_s.at[k], recv_sem=map_r.at[k],
            device_id=(source, t), device_id_type=MESH,
        )

    lax.fori_loop(1, REP, lambda k, c: (map_to(k).start(), c)[1], 0)
    own_map = pltpu.make_async_copy(map_ref, holders_out.at[place.r], local.at[5])
    own_map.start()
    own = pltpu.make_async_copy(
        own_rows.at[:, pl.ds(pl.multiple_of(t * SHARE, SHARE), SHARE)],
        spread.at[pl.ds(pl.multiple_of(t * OWN, OWN), OWN), :],
        local.at[2],
    )
    own.start()
    own.wait()
    lax.fori_loop(1, TP, lambda k, c: (share_from(k).wait_recv(), c)[1], 0)

    slots = slots_ref[...]
    found = jnp.zeros((TOK, SHARE), F32)
    block = 512
    for b in range(TP * OWN // block):
        places = lax.broadcasted_iota(jnp.int32, (TOK, block), 1) + b * block
        one_hot = jnp.where(slots == places, 1.0, 0.0).astype(BF16)
        found += jnp.dot(one_hot, spread[b * block : (b + 1) * block, :], preferred_element_type=F32)
    inputs[t] = found.astype(BF16)

    def input_view(chunk, low, count):
        return inputs.at[chunk, pl.ds(low, count), :]

    tree = Tree(input_view, place.tp_ids, place.tp_dev, tree_s, tree_r, TOK, 224)
    sibs = Siblings(tree, input_view, TOK, place, sib_s, sib_r)
    tree.begin()
    sibs.start("me")
    load_weight.wait()

    def multiplied(chunk, first=False):
        depth = pl.ds(pl.multiple_of(chunk * SHARE, SHARE), SHARE)
        for n in range(4):
            cols = slice(n * 256, (n + 1) * 256)
            part = jnp.dot(inputs[chunk], weight[depth, cols], preferred_element_type=F32)
            total[:, cols] = part if first else total[:, cols] + part

    multiplied(t, True)
    waiting = ["me"]

    def whole(name):
        sibs.start(name)
        multiplied(tree.names[name])
        before = waiting.pop()
        sibs.wait(before)
        multiplied(tree.names[before] + 1 - 2 * place.core)
        waiting.append(name)

    for step in tree.steps(whole):
        step()
    sibs.wait(waiting[0])
    multiplied(tree.names[waiting[0]] + 1 - 2 * place.core)

    store_inputs = pltpu.make_async_copy(inputs, inputs_out, local.at[3])
    store_inputs.start()

    def gate_rows(n, carry):
        at = pl.ds(pl.multiple_of(n * 16, 16), 16)
        gate = total[at, :] * SCALING
        logistic = 1.0 / (1.0 + jnp.exp(-gate))
        grad[at, :] = (
            upstream_ref[at, :].astype(F32) * act_ref[at, :].astype(F32) * logistic * (1.0 + gate * (1.0 - logistic))
        ).astype(BF16)
        return carry

    lax.fori_loop(0, TOK // 16, gate_rows, 0)
    pieces[t] = grad[:, WIDE:]

    def piece_view(chunk, low, count):
        return pieces.at[chunk, pl.ds(low, count), :]

    tree2 = Tree(piece_view, place.tp_ids, place.tp_dev, tree2_s, tree2_r, TOK, 224)
    sibs2 = Siblings(tree2, piece_view, TOK, place, sib2_s, sib2_r)
    tree2.begin()
    sibs2.start("me")
    for step in tree2.steps(sibs2.start):
        step()
    for name in ORDER:
        sibs2.wait(name)

    own_entry = holders_ref[0, t]
    for s in range(SEVEN):
        wanted = t * SEVEN + s
        owner = jnp.int32(0)
        for other in range(TP):
            owner = jnp.where(holders_ref[0, other] == wanted, other, owner)
        cols = slice(s * UNIT, (s + 1) * UNIT)
        grad[:, cols] = jnp.where(own_entry == -2, pieces[owner], grad[:, cols])
    store_grad = pltpu.make_async_copy(grad.at[:, pl.ds(0, WIDE)], grad_out, local.at[4])
    store_grad.start()

    lax.fori_loop(1, TP, lambda k, c: (share_to(k).wait_send(), c)[1], 0)
    for book in (tree, sibs, tree2, sibs2):
        book.drain()
    own_map.wait()
    lax.fori_loop(1, REP, lambda k, c: (map_from(k).wait_recv(), c)[1], 0)
    lax.fori_loop(1, REP, lambda k, c: (map_to(k).wait_send(), c)[1], 0)
    store_inputs.wait()
    store_grad.wait()


def back_kernel(
    inputs_ref, grad_ref, holders_ref, master_ref, one_ref, two_ref,
    master_out, one_out, two_out, full_out, adopted_out,
    parts, grads, total, fresh, strips, spread, picked, routed, adopted, master, one, two,
    swap_s, swap_r, part_s, part_r, sib_s, sib_r, grad_s, grad_r, fresh_s, fresh_r,
    p1_s, p1_r, p2_s, p2_r, p3_s, p3_r, local, outs,
):
    place = Place()
    r, t = place.r, place.t
    load_grad = pltpu.make_async_copy(grad_ref, grads.at[r], local.at[0])
    load_grad.start()
    loads = [
        pltpu.make_async_copy(a, b, local.at[n + 1])
        for n, (a, b) in enumerate(((master_ref, master), (one_ref, one), (two_ref, two)))
    ]
    for load in loads:
        load.start()
    greet(place)

    mine_rows = pl.ds(pl.multiple_of(place.chip * PART, PART), PART)
    mine_cols = pl.ds(pl.multiple_of(place.core * SHARE, SHARE), SHARE)

    def swap_to(k):
        to = (r + k) % REP
        return pltpu.make_async_remote_copy(
            src_ref=inputs_ref.at[2 * to + place.core, mine_rows, :],
            dst_ref=parts.at[r, mine_rows, mine_cols],
            send_sem=swap_s.at[k], recv_sem=swap_r.at[k], device_id=(to, t), device_id_type=MESH,
        )

    def swap_from(k):
        source = (r + REP - k) % REP
        ref = parts.at[source, mine_rows, mine_cols]
        return pltpu.make_async_remote_copy(
            src_ref=ref, dst_ref=ref, send_sem=swap_s.at[k], recv_sem=swap_r.at[k],
            device_id=(source, t), device_id_type=MESH,
        )

    lax.fori_loop(1, REP, lambda k, c: (swap_to(k).start(), c)[1], 0)
    own = pltpu.make_async_copy(
        inputs_ref.at[2 * r + place.core, mine_rows, :], parts.at[r, mine_rows, mine_cols], local.at[4]
    )
    own.start()

    def grad_view(chunk, low, count):
        return grads.at[chunk, pl.ds(low, count), :]

    load_grad.wait()
    gtree = Tree(grad_view, place.rep_ids, place.rep_dev, grad_s, grad_r, TOK, 224)
    gtree.begin()

    def part_view(chunk, low, count):
        at, side = chunk // 2, chunk % 2
        return parts.at[
            pl.ds(low, count),
            pl.ds(pl.multiple_of(at * PART, PART), PART),
            pl.ds(pl.multiple_of(side * SHARE, SHARE), SHARE),
        ]

    own.wait()
    lax.fori_loop(1, REP, lambda k, c: (swap_from(k).wait_recv(), c)[1], 0)
    ptree = Tree(part_view, place.tp_ids, place.tp_dev, part_s, part_r, REP, REP)
    sibs = Siblings(ptree, part_view, REP, place, sib_s, sib_r)
    ptree.begin()
    sibs.start("me")

    def multiplied(chunk, first=False):
        part = lax.dot_general(
            parts[chunk], grads[chunk], (((0,), (0,)), ((), ())), preferred_element_type=F32
        )
        total[...] = part if first else total[...] + part

    ready = []
    gsteps = gtree.steps(lambda name: multiplied(gtree.names[name]))
    gsteps[0]()
    for step in ptree.steps(sibs.start):
        step()
    for name in ORDER:
        sibs.wait(name)
    multiplied(r, True)
    for step in gsteps[1:]:
        step()

    for load in loads:
        load.wait()

    def adam_rows(n, carry):
        at = pl.ds(pl.multiple_of(n * 16, 16), 16)
        gradient = total[at, :] * SCALING
        first_new = beta_one * one[at, :].astype(F32) + (1.0 - beta_one) * gradient
        second_new = beta_two * two[at, :].astype(F32) + (1.0 - beta_two) * gradient * gradient
        step_size = first_new / bias_one / (jnp.sqrt(second_new / bias_two) + epsilon)
        old = master[at, :]
        new = old - learn_rate * (step_size + weight_decay * old)
        master[at, :] = new
        one[at, :] = first_new.astype(BF16)
        two[at, :] = second_new.astype(BF16)
        low = new.astype(BF16)
        fresh[r, at, :] = low
        for s in range(SEVEN):
            strips[s, at, :] = low[:, s * UNIT : (s + 1) * UNIT]
        return carry

    lax.fori_loop(0, ROWS // 16, adam_rows, 0)

    def fresh_view(chunk, low, count):
        return fresh.at[chunk, pl.ds(low, count), :]

    ftree = Tree(fresh_view, place.rep_ids, place.rep_dev, fresh_s, fresh_r, ROWS, 384)

    def one_to(k):
        to = (t + k) % TP
        return pltpu.make_async_remote_copy(
            src_ref=strips.at[:, pl.ds(pl.multiple_of(to * STRIP, STRIP), STRIP), :],
            dst_ref=spread.at[pl.ds(t * SEVEN, SEVEN)],
            send_sem=p1_s.at[k], recv_sem=p1_r.at[k], device_id=(r, to), device_id_type=MESH,
        )

    def one_from(k):
        source = (t + TP - k) % TP
        ref = spread.at[pl.ds(source * SEVEN, SEVEN)]
        return pltpu.make_async_remote_copy(
            src_ref=ref, dst_ref=ref, send_sem=p1_s.at[k], recv_sem=p1_r.at[k],
            device_id=(r, source), device_id_type=MESH,
        )

    lax.fori_loop(1, TP, lambda k, c: (one_to(k).start(), c)[1], 0)
    ftree.begin()
    spread[pl.ds(t * SEVEN, SEVEN)] = strips[:, pl.ds(pl.multiple_of(t * STRIP, STRIP), STRIP), :]
    stores = [
        pltpu.make_async_copy(a, b, outs.at[n])
        for n, (a, b) in enumerate(((master, master_out), (one, one_out), (two, two_out), (fresh.at[r], full_out.at[r])))
    ]
    for store in stores:
        store.start()

    lax.fori_loop(1, TP, lambda k, c: (one_from(k).wait_recv(), c)[1], 0)

    def pick(n, carry):
        q, to = n // TP, n % TP
        piece = holders_ref[q, 0, to]
        value = spread[jnp.maximum(piece, 0)]
        picked[to, q] = jnp.where(piece >= 0, value, jnp.zeros_like(value))
        return carry

    lax.fori_loop(0, REP * TP, pick, 0)

    def two_to(k):
        to = (t + k) % TP
        return pltpu.make_async_remote_copy(
            src_ref=picked.at[to], dst_ref=routed.at[:, pl.ds(pl.multiple_of(t * STRIP, STRIP), STRIP), :],
            send_sem=p2_s.at[k], recv_sem=p2_r.at[k], device_id=(r, to), device_id_type=MESH,
        )

    def two_from(k):
        source = (t + TP - k) % TP
        ref = routed.at[:, pl.ds(pl.multiple_of(source * STRIP, STRIP), STRIP), :]
        return pltpu.make_async_remote_copy(
            src_ref=ref, dst_ref=ref, send_sem=p2_s.at[k], recv_sem=p2_r.at[k],
            device_id=(r, source), device_id_type=MESH,
        )

    lax.fori_loop(1, TP, lambda k, c: (two_to(k).start(), c)[1], 0)
    routed[:, pl.ds(pl.multiple_of(t * STRIP, STRIP), STRIP), :] = picked[t]

    def stored(name):
        chunk = ftree.names[name]
        store = pltpu.make_async_copy(fresh.at[chunk], full_out.at[chunk], outs.at[4 + ORDER.index(name)])
        store.start()
        stores.append(store)

    fsteps = ftree.steps(stored)
    for step in fsteps[:3]:
        step()

    lax.fori_loop(1, TP, lambda k, c: (two_from(k).wait_recv(), c)[1], 0)

    def three_to(k):
        to = (r + k) % REP
        return pltpu.make_async_remote_copy(
            src_ref=routed.at[to], dst_ref=adopted.at[r], send_sem=p3_s.at[k], recv_sem=p3_r.at[k],
            device_id=(to, t), device_id_type=MESH,
        )

    def three_from(k):
        source = (r + REP - k) % REP
        return pltpu.make_async_remote_copy(
            src_ref=adopted.at[source], dst_ref=adopted.at[source], send_sem=p3_s.at[k], recv_sem=p3_r.at[k],
            device_id=(source, t), device_id_type=MESH,
        )

    lax.fori_loop(1, REP, lambda k, c: (three_to(k).start(), c)[1], 0)
    adopted[r] = routed[r]
    for step in fsteps[3:]:
        step()
    lax.fori_loop(1, REP, lambda k, c: (three_from(k).wait_recv(), c)[1], 0)
    store = pltpu.make_async_copy(adopted, adopted_out, outs.at[12])
    store.start()
    stores.append(store)

    for book in (ptree, sibs, gtree, ftree):
        book.drain()
    lax.fori_loop(1, REP, lambda k, c: (swap_to(k).wait_send(), c)[1], 0)
    lax.fori_loop(1, TP, lambda k, c: (one_to(k).wait_send(), c)[1], 0)
    lax.fori_loop(1, TP, lambda k, c: (two_to(k).wait_send(), c)[1], 0)
    lax.fori_loop(1, REP, lambda k, c: (three_to(k).wait_send(), c)[1], 0)
    for store in stores:
        store.wait()


ANY = pl.BlockSpec(memory_space=pl.ANY)
VM = pl.BlockSpec(memory_space=pltpu.VMEM)
SM = pl.BlockSpec(memory_space=pltpu.SMEM)


def sems(*counts):
    return [pltpu.SemaphoreType.DMA((n,)) for n in counts for _ in (0, 1)]


def on_device(
    batch_rows, token_slots, holder_map, copies, upstream, up_act, master, moment1, moment2
):
    own_entry = jnp.sum(jnp.where(jnp.arange(TP) == lax.axis_index("tp"), holder_map[0], 0))
    inputs, block_grad, all_holders = pl.pallas_call(
        front_kernel,
        out_shape=(
            jax.ShapeDtypeStruct((TP, TOK, SHARE), BF16),
            jax.ShapeDtypeStruct((TOK, WIDE), BF16),
            jax.ShapeDtypeStruct((REP, 1, TP), jnp.int32),
        ),
        in_specs=[ANY, VM, SM, ANY, ANY, VM, VM],
        out_specs=(ANY, ANY, ANY),
        scratch_shapes=[
            pltpu.VMEM((OWN, D), BF16),
            pltpu.VMEM((TP * OWN, SHARE), BF16),
            pltpu.VMEM((TP, TOK, SHARE), BF16),
            pltpu.VMEM((D, NARROW), BF16),
            pltpu.VMEM((TOK, NARROW), F32),
            pltpu.VMEM((TOK, NARROW), BF16),
            pltpu.VMEM((TP, TOK, UNIT), BF16),
            *sems(REP, TP, 13, 8, 13, 8),
            pltpu.SemaphoreType.DMA((6,)),
        ],
        compiler_params=pltpu.CompilerParams(
            collective_id=0, has_side_effects=True, vmem_limit_bytes=56 << 20
        ),
        name="front",
    )(batch_rows, token_slots.reshape(TOK, 1), holder_map, holder_map, copies, upstream, up_act)
    master_next, one_next, two_next, full, adopted = pl.pallas_call(
        back_kernel,
        out_shape=(
            jax.ShapeDtypeStruct((ROWS, WIDE), F32),
            jax.ShapeDtypeStruct((ROWS, WIDE), BF16),
            jax.ShapeDtypeStruct((ROWS, WIDE), BF16),
            jax.ShapeDtypeStruct((REP, ROWS, WIDE), BF16),
            jax.ShapeDtypeStruct((REP, ROWS, UNIT), BF16),
        ),
        in_specs=[ANY, ANY, SM, ANY, ANY, ANY],
        out_specs=(ANY,) * 5,
        scratch_shapes=[
            pltpu.VMEM((REP, TOK, ROWS), BF16),
            pltpu.VMEM((REP, TOK, WIDE), BF16),
            pltpu.VMEM((ROWS, WIDE), F32),
            pltpu.VMEM((REP, ROWS, WIDE), BF16),
            pltpu.VMEM((SEVEN, ROWS, UNIT), BF16),
            pltpu.VMEM((TP * SEVEN, STRIP, UNIT), BF16),
            pltpu.VMEM((TP, REP, STRIP, UNIT), BF16),
            pltpu.VMEM((REP, ROWS, UNIT), BF16),
            pltpu.VMEM((REP, ROWS, UNIT), BF16),
            pltpu.VMEM((ROWS, WIDE), F32),
            pltpu.VMEM((ROWS, WIDE), BF16),
            pltpu.VMEM((ROWS, WIDE), BF16),
            *sems(REP, 13, 8, 13, 13, TP, TP, REP),
            pltpu.SemaphoreType.DMA((5,)),
            pltpu.SemaphoreType.DMA((13,)),
        ],
        compiler_params=pltpu.CompilerParams(
            collective_id=1, has_side_effects=True, vmem_limit_bytes=56 << 20
        ),
        name="back",
    )(inputs, block_grad, all_holders, master, moment1, moment2)
    copy_next = jnp.concatenate([full.reshape(D, WIDE), adopted.reshape(D, UNIT)], axis=1)
    copy_next = jnp.where(own_entry == -2, jnp.zeros_like(copy_next), copy_next)
    return master_next, one_next, two_next, copy_next


def solution(mesh):
    placed = (
        P(("rep", "tp"), None),
        P("rep", None),
        P("rep", None),
        P("rep", "tp"),
        P("rep", "tp"),
        P("rep", "tp"),
        P("rep", "tp"),
        P("rep", "tp"),
        P("rep", "tp"),
    )
    return jax.shard_map(
        on_device,
        mesh=mesh,
        in_specs=placed,
        out_specs=(P("rep", "tp"), P("rep", "tp"), P("rep", "tp"), P("rep", "tp")),
        check_vma=False,
    )
```

time: 367 us -> 223 us (0.61)
  waiting for transfers between devices: 232 us -> 0 us
  Pallas kernels: 0 us -> 207 us
  blocking collectives: 61.1 us -> 0 us
  starting transfers between devices: 18.8 us -> 0 us
  matrix products: 16.4 us -> 0 us
  between operations: 14.6 us -> 1.33 us
  other arithmetic: 17.5 us -> 9.24 us
    pallas_call x0 -> x2, Pallas kernels: none -> 207 us  [the longest x1 150 us: on_device(): pl.pallas_call(back_kernel, out_shape=(jax.ShapeDtypeStruct((ROWS, WIDE),...]
    all_to_all x3 -> x0, waiting for transfers between devices: 98 us -> none  [the longest x1 60.8 us: on_device(): lax.all_to_all(fresh, 'tp', split_axis=0, concat_axis=0, tiled=True)]
    reduce_scatter x1 -> x0, waiting for transfers between devices: 81.7 us -> none  [on_device(): lax.psum_scatter((product * scaling).astype(jnp.bfloat16), 'rep', scatter...]
    all_gather x2 -> x0, waiting for transfers between devices: 51.7 us -> none  [the longest x1 51.7 us: on_device(): inputs = lax.all_gather(chosen, 'tp', axis=1, tiled=True)]
    all_to_all x2 -> x0, blocking collectives: 40.4 us -> none  [the longest x1 22.6 us: on_device(): lax.all_to_all(routed, 'tp', split_axis=1, concat_axis=2, tiled=True)]
    all_gather x1 -> x0, blocking collectives: 20.7 us -> none  [on_device(): all_holders = lax.all_gather(holders, 'rep')]
    all_to_all x3 -> x0, starting transfers between devices: 18.7 us -> none  [the longest x1 8.1 us: on_device(): lax.all_to_all(batch_rows, 'tp', split_axis=1, concat_axis=0, tiled=True)]
    dot_general x4 -> x0, matrix products: 16.4 us -> none  [the longest x1 8.27 us: on_device(): jnp.dot(inputs, copies, preferred_element_type=jnp.float32) * scaling]
  transfers between devices with their start and end apart: 6 -> 0, of which waited for: 5 -> 0; matrix products, arithmetic and copies ran while one was open for 1% -> 0% of each run, Pallas kernels for 0% -> 0%
where the time goes in v2:
time: 223 us; the launch traced here: 222 us
  Pallas kernels  207 us (93%)
  other arithmetic  9.24 us (4%)
  local copies, waits for them, and re-layouts  4.59 us (2%)
    pallas_call x1, Pallas kernels, on_device(): pl.pallas_call(back_kernel, out_shape=(jax.ShapeDtypeStruct((ROWS, WIDE),...  150 us
    pallas_call x1, Pallas kernels, on_device(): pl.pallas_call(front_kernel, out_shape=(jax.ShapeDtypeStruct((TP, TOK, SH...  57 us
    select_n x1, other arithmetic, on_device(): copy_next = jnp.where(own_entry == -2, jnp.zeros_like(copy_next), copy_next)  7.94 us

profile of v2, /device:TPU:0, one launch (start us, length us, event | category | flops | bytes accessed | tf_op | source)
XLA Modules:
  0.0 222.2 jit_solution(2444137284237796361)
XLA Ops:
  0.6 1.3 fusion
  2.6 1.5 copy.13.slots_ref
  4.1 57.0 %front.1 = (bf16[16,384,256]{2,1,0:T(8,128)(2,1)}, bf16[384,896]{1,0:T(8,128)(2,1)}, s32[8,1,16]{2,1,0:T(1,128)}) custom-call(bf16[96,4096]{1,0:T(8,128)(2,1)} %rows_ref.1, s32[384,1]{1,0:T(8,128)} %copy.13.slots_ref, s32[1,16]{1,0:T(1,128)} %map_ref.1, s32[1,16]{1,0:T(1,128)} %map_ref.1, bf16[4096,1024]{1,0:T(8,128)(2,1)} %copies_ref.1, ...), custom_call_target="tpu_custom_call" | custom-call | tf_op jit(solution)/shard_map/front/pallas_call | solution.py:561
  61.1 150.0 %back.1 = (f32[512,896]{1,0:T(8,128)}, bf16[512,896]{1,0:T(8,128)(2,1)}, bf16[512,896]{1,0:T(8,128)(2,1)}, bf16[8,512,896]{2,1,0:T(8,128)(2,1)}, bf16[8,512,128]{2,1,0:T(8,128)(2,1)}) custom-call(bf16[16,384,256]{2,1,0:T(8,128)(2,1)} %get-tuple-element.12.inputs_ref, bf16[384,896]{1,0:T(8,128)(2,1)} %get-tuple-element.13.grad_ref, ...), custom_call_target="tpu_custom_call" | custom-call | tf_op jit(solution)/shard_map/back/pallas_call | solution.py:586
  211.1 0.0 copy-start
  211.1 0.0 copy-start.2
  211.1 0.0 copy-start.1
  211.1 7.9 %maximum_select_fusion = bf16[4096,1024]{1,0:T(8,128)(2,1)} fusion(bf16[4096,128]{1,0:T(8,128)(2,1)} %bitcast.6, bf16[4096,896]{1,0:T(8,128)(2,1)} %bitcast.5, pred[]{:T(512)S(6)} %eq.11), kind=kLoop, calls=%fused_computation | loop fusion | flops 20971520 | bytes 16777216 | tf_op jit(solution)/shard_map/jit(_where)/select_n | solution.py:620
  219.1 0.0 copy-done
  219.1 1.2 copy.17
  220.3 0.0 copy-done.2
  220.3 0.9 copy.18
  221.2 0.0 copy-done.1
  221.2 0.9 copy.19
Async XLA Ops:
  211.1 8.0 %copy-start = (f32[512,896]{1,0:T(8,128)S(1)}, f32[512,896]{1,0:T(8,128)}, u32[]{:S(2)}) copy-start(f32[512,896]{1,0:T(8,128)} %get-tuple-element.24) | copy-start | bytes 5505028
  211.1 9.2 %copy-start.2 = (bf16[512,896]{1,0:T(8,128)(2,1)S(1)}, bf16[512,896]{1,0:T(8,128)(2,1)}, u32[]{:S(2)}) copy-start(bf16[512,896]{1,0:T(8,128)(2,1)} %get-tuple-element.25) | copy-start | bytes 2752516
  211.1 10.1 %copy-start.1 = (bf16[512,896]{1,0:T(8,128)(2,1)S(1)}, bf16[512,896]{1,0:T(8,128)(2,1)}, u32[]{:S(2)}) copy-start(bf16[512,896]{1,0:T(8,128)(2,1)} %get-tuple-element.26) | copy-start | bytes 2752516

commit v3 on v2

v3 whole, which is shorter than its diff:
```python
import functools
import math

import jax
import jax.numpy as jnp
from jax import lax
from jax.experimental import pallas as pl
from jax.experimental.pallas import tpu as pltpu
from jax.sharding import PartitionSpec as P

beta_one = 0.9
beta_two = 0.95
bias_one = 1.0 - 0.9**10
bias_two = 1.0 - 0.95**10
learn_rate = 0.05
weight_decay = 0.1
epsilon = 1e-08

D, TOK, WIDE, UNIT, NARROW = 4096, 384, 896, 128, 1024
REP, TP = 8, 16
OWN, SHARE = 96, 256
ROWS = D // REP
STRIP = ROWS // TP
SEVEN = WIDE // UNIT
PART = TOK // (TP // 2)
KINDS = REP // 2
SCALING = 1.0 / math.sqrt(D)
MESH = pl.DeviceIdType.MESH
F32, BF16 = jnp.float32, jnp.bfloat16


class Place:
    def __init__(self):
        r, t = lax.axis_index("rep"), lax.axis_index("tp")
        self.r, self.t = r, t
        x, zl = r % 4, r // 4
        y, zh, c = t // 4, (t // 2) % 2, t % 2
        self.core = c
        self.chip = t // 2
        self.sibling = (r, t + 1 - 2 * c)

        def rep_id(step, flip):
            return (x + step) % 4 + 4 * ((zl + flip) % 2)

        def tp_id(step, flip):
            return ((y + step) % 4) * 4 + ((zh + flip) % 2) * 2 + c

        self.rep_ids = [[rep_id(s, f) for s in (0, 1, 3, 2)] for f in (0, 1)]
        self.tp_ids = [[tp_id(s, f) for s in (0, 1, 3, 2)] for f in (0, 1)]

    def rep_dev(self, other):
        return (other, self.t)

    def tp_dev(self, other):
        return (self.r, other)


def greet(place):
    barrier = pltpu.get_barrier_semaphore()

    def rep_mate(k, carry):
        pl.semaphore_signal(barrier, inc=1, device_id=((place.r + k) % REP, place.t), device_id_type=MESH)
        return carry

    def tp_mate(k, carry):
        pl.semaphore_signal(barrier, inc=1, device_id=(place.r, (place.t + k) % TP), device_id_type=MESH)
        return carry

    lax.fori_loop(1, REP, rep_mate, 0)
    lax.fori_loop(1, TP, tp_mate, 0)
    pl.semaphore_wait(barrier, REP + TP - 2)


class Tree:
    def __init__(self, view, ids, dev, ssem, rsem, extent, first):
        (me, nx, pv, op), (me_p, nx_p, pv_p, op_p) = ids
        to_nx, to_pv, to_pair = dev(nx), dev(pv), dev(me_p)
        half, a_half, rest = extent // 2, first // 2, extent - first
        self.rest, self.names = rest, dict(me=me, nx=nx, pv=pv, op=op, me_p=me_p, nx_p=nx_p, pv_p=pv_p, op_p=op_p)
        sent = {
            1: (me, 0, extent, to_nx), 2: (me, 0, extent, to_pv), 3: (me, 0, first, to_pair), 4: (me, first, rest, to_pair),
            5: (me_p, 0, first, to_nx), 6: (me_p, 0, first, to_pv), 7: (pv, 0, half, to_nx), 8: (nx, half, half, to_pv),
            9: (pv_p, 0, a_half, to_nx), 10: (nx_p, a_half, a_half, to_pv),
            11: (pv, first, rest, to_pair), 12: (nx, first, rest, to_pair), 13: (op, first, rest, to_pair),
        }
        got = {1: pv, 2: nx, 3: me_p, 4: me_p, 5: pv_p, 6: nx_p, 7: op, 8: op, 9: op_p, 10: op_p, 11: pv_p, 12: nx_p, 13: op_p}
        skipped = () if rest else (4, 11, 12, 13)
        self.out, self.into = {}, {}
        for i, (chunk, low, count, to) in sent.items():
            if i not in skipped:
                for book, which in ((self.out, chunk), (self.into, got[i])):
                    ref = view(which, low, count)
                    book[i] = pltpu.make_async_remote_copy(
                        src_ref=ref, dst_ref=ref, send_sem=ssem.at[i - 1], recv_sem=rsem.at[i - 1],
                        device_id=to, device_id_type=MESH,
                    )

    def start(self, *which):
        for i in which:
            if i in self.out:
                self.out[i].start()

    def wait(self, *which):
        for i in which:
            if i in self.into:
                self.into[i].wait_recv()

    def steps(self, done):
        def pair():
            self.wait(3)
            self.start(5, 6)
            if not self.rest:
                done("me_p")

        def previous():
            self.wait(1)
            self.start(7, 11)
            done("pv")

        def following():
            self.wait(2)
            self.start(8, 12)
            done("nx")

        def pair_previous():
            self.wait(5)
            self.start(9)
            if not self.rest:
                done("pv_p")

        def pair_following():
            self.wait(6)
            self.start(10)
            if not self.rest:
                done("nx_p")

        def opposite():
            self.wait(7, 8)
            self.start(13)
            done("op")

        def rests():
            if self.rest:
                self.wait(4)
                done("me_p")
                self.wait(11)
                done("pv_p")
                self.wait(12)
                done("nx_p")

        def last():
            self.wait(9, 10, 13)
            done("op_p")

        return [pair, previous, following, pair_previous, pair_following, opposite, rests, last]

    def begin(self):
        self.start(3, 1, 2, 4)

    def drain(self):
        for copy in self.out.values():
            copy.wait_send()


ORDER = ("me", "pv", "nx", "me_p", "op", "pv_p", "nx_p", "op_p")


class Siblings:
    def __init__(self, tree, view, extent, place, ssem, rsem):
        self.out, self.into = {}, {}
        for n, name in enumerate(ORDER):
            mine = tree.names[name]
            for book, which in ((self.out, mine), (self.into, mine + 1 - 2 * place.core)):
                ref = view(which, 0, extent)
                book[name] = pltpu.make_async_remote_copy(
                    src_ref=ref, dst_ref=ref, send_sem=ssem.at[n], recv_sem=rsem.at[n],
                    device_id=place.sibling, device_id_type=MESH,
                )

    def start(self, name):
        self.out[name].start()

    def wait(self, name):
        self.into[name].wait_recv()

    def drain(self):
        for copy in self.out.values():
            copy.wait_send()


def step_kernel(
    rows_ref, slots_ref, holders_ref, map_ref, copies_ref, upstream_ref, act_ref, master_ref, one_ref, two_ref,
    master_out, one_out, two_out, full_out, adopted_out, maps_out,
    own_rows, spread, inputs, weight, gates, upstream, act, grad, pieces,
    parts, grads, total, fresh, strips, strewn, picked, routed, outgoing, adopted, master, one, two, maps,
    map_s, map_r, row_s, row_r, tree_s, tree_r, sib_s, sib_r, tree2_s, tree2_r, sib2_s, sib2_r,
    swap_s, swap_r, part_s, part_r, sib3_s, sib3_r, grad_s, grad_r, fresh_s, fresh_r,
    p1_s, p1_r, p2_s, p2_r, p3_s, p3_r, local, outs,
):
    place = Place()
    r, t = place.r, place.t

    def loading(n, source, target):
        copy = pltpu.make_async_copy(source, target, local.at[n])
        copy.start()
        return copy

    load_rows = loading(0, rows_ref, own_rows)
    load_weight = loading(1, copies_ref, weight)
    load_factors = [loading(2, upstream_ref, upstream), loading(3, act_ref, act)]
    load_state = [loading(4, master_ref, master), loading(5, one_ref, one), loading(6, two_ref, two)]
    own_map = loading(7, map_ref, maps_out.at[r])
    greet(place)
    load_rows.wait()

    def each(count, act_on):
        lax.fori_loop(1, count, lambda k, c: (act_on(k), c)[1], 0)

    def remote(source, target, s, r_, k, to):
        return pltpu.make_async_remote_copy(
            src_ref=source, dst_ref=target, send_sem=s.at[k], recv_sem=r_.at[k], device_id=to, device_id_type=MESH
        )

    def share_to(k):
        to = (t + k) % TP
        return remote(
            own_rows.at[:, pl.ds(pl.multiple_of(to * SHARE, SHARE), SHARE)],
            spread.at[pl.ds(pl.multiple_of(t * OWN, OWN), OWN), :], row_s, row_r, k, (r, to),
        )

    def share_from(k):
        source = (t + TP - k) % TP
        ref = spread.at[pl.ds(pl.multiple_of(source * OWN, OWN), OWN), :]
        return remote(ref, ref, row_s, row_r, k, (r, source))

    each(TP, lambda k: share_to(k).start())
    own_share = loading(
        8, own_rows.at[:, pl.ds(pl.multiple_of(t * SHARE, SHARE), SHARE)],
        spread.at[pl.ds(pl.multiple_of(t * OWN, OWN), OWN), :],
    )

    def map_to(k):
        return remote(map_ref, maps_out.at[r], map_s, map_r, k, ((r + k) % REP, t))

    def map_from(k):
        source = (r + REP - k) % REP
        return remote(map_ref, maps_out.at[source], map_s, map_r, k, (source, t))

    each(REP, lambda k: map_to(k).start())
    own_share.wait()
    each(TP, lambda k: share_from(k).wait_recv())

    slots = slots_ref[...]
    found = jnp.zeros((TOK, SHARE), F32)
    block = 512
    for b in range(TP * OWN // block):
        places = lax.broadcasted_iota(jnp.int32, (TOK, block), 1) + b * block
        one_hot = jnp.where(slots == places, 1.0, 0.0).astype(BF16)
        found += jnp.dot(one_hot, spread[b * block : (b + 1) * block, :], preferred_element_type=F32)
    inputs[t] = found.astype(BF16)

    def input_view(chunk, low, count):
        return inputs.at[chunk, pl.ds(low, count), :]

    tree = Tree(input_view, place.tp_ids, place.tp_dev, tree_s, tree_r, TOK, 224)
    sibs = Siblings(tree, input_view, TOK, place, sib_s, sib_r)
    tree.begin()
    sibs.start("me")
    load_weight.wait()

    def multiplied(chunk, first=False):
        depth = pl.ds(pl.multiple_of(chunk * SHARE, SHARE), SHARE)
        for n in range(4):
            cols = slice(n * 256, (n + 1) * 256)
            part = jnp.dot(inputs[chunk], weight[depth, cols], preferred_element_type=F32)
            gates[:, cols] = part if first else gates[:, cols] + part

    def other_multiplied(name):
        sibs.wait(name)
        multiplied(tree.names[name] + 1 - 2 * place.core)

    multiplied(t, True)
    waiting = ["me"]

    def whole(name):
        sibs.start(name)
        multiplied(tree.names[name])
        waiting.append(name)
        if len(waiting) > 2:
            other_multiplied(waiting.pop(0))

    for step in tree.steps(whole):
        step()
    for name in waiting:
        other_multiplied(name)

    mine_rows = pl.ds(pl.multiple_of(place.chip * PART, PART), PART)
    mine_cols = pl.ds(pl.multiple_of(place.core * SHARE, SHARE), SHARE)

    def swap_to(k):
        to = (r + k) % REP
        return remote(
            inputs.at[2 * to + place.core, mine_rows, :], parts.at[r, mine_rows, mine_cols], swap_s, swap_r, k, (to, t)
        )

    def swap_from(k):
        source = (r + REP - k) % REP
        ref = parts.at[source, mine_rows, mine_cols]
        return remote(ref, ref, swap_s, swap_r, k, (source, t))

    each(REP, lambda k: swap_to(k).start())
    own_swap = loading(9, inputs.at[2 * r + place.core, mine_rows, :], parts.at[r, mine_rows, mine_cols])

    for load in load_factors:
        load.wait()

    def gate_rows(n, carry):
        at = pl.ds(pl.multiple_of(n * 16, 16), 16)
        gate = gates[at, :] * SCALING
        logistic = 1.0 / (1.0 + jnp.exp(-gate))
        grad[at, :] = (
            upstream[at, :].astype(F32) * act[at, :].astype(F32) * logistic * (1.0 + gate * (1.0 - logistic))
        ).astype(BF16)
        return carry

    lax.fori_loop(0, TOK // 16, gate_rows, 0)
    pieces[t] = grad[:, WIDE:]

    def piece_view(chunk, low, count):
        return pieces.at[chunk, pl.ds(low, count), :]

    tree2 = Tree(piece_view, place.tp_ids, place.tp_dev, tree2_s, tree2_r, TOK, TOK)
    sibs2 = Siblings(tree2, piece_view, TOK, place, sib2_s, sib2_r)
    tree2.begin()
    sibs2.start("me")
    for step in tree2.steps(sibs2.start):
        step()
    own_swap.wait()
    each(REP, lambda k: swap_from(k).wait_recv())
    for name in ORDER:
        sibs2.wait(name)

    own_entry = holders_ref[0, t]
    for s in range(SEVEN):
        wanted = t * SEVEN + s
        owner = jnp.int32(0)
        for other in range(TP):
            owner = jnp.where(holders_ref[0, other] == wanted, other, owner)
        cols = slice(s * UNIT, (s + 1) * UNIT)
        grads[r, :, cols] = jnp.where(own_entry == -2, pieces[owner], grad[:, cols])

    def grad_view(chunk, low, count):
        return grads.at[chunk, pl.ds(low, count), :]

    gtree = Tree(grad_view, place.rep_ids, place.rep_dev, grad_s, grad_r, TOK, 224)
    gtree.begin()

    def part_view(chunk, low, count):
        at, side = chunk // 2, chunk % 2
        return parts.at[
            pl.ds(low, count),
            pl.ds(pl.multiple_of(at * PART, PART), PART),
            pl.ds(pl.multiple_of(side * SHARE, SHARE), SHARE),
        ]

    ptree = Tree(part_view, place.tp_ids, place.tp_dev, part_s, part_r, REP, REP)
    sibs3 = Siblings(ptree, part_view, REP, place, sib3_s, sib3_r)
    ptree.begin()
    sibs3.start("me")

    def gathered(chunk, first=False):
        part = lax.dot_general(
            parts[chunk], grads[chunk], (((0,), (0,)), ((), ())), preferred_element_type=F32
        )
        total[...] = part if first else total[...] + part

    own_map.wait()
    each(REP, lambda k: map_from(k).wait_recv())
    load_maps = loading(10, maps_out, maps)
    gsteps = gtree.steps(lambda name: gathered(gtree.names[name]))
    psteps = ptree.steps(sibs3.start)
    for step in psteps[:5]:
        step()
    gsteps[0]()
    for step in psteps[5:]:
        step()
    for name in ORDER:
        sibs3.wait(name)
    gathered(r, True)
    for step in gsteps[1:]:
        step()

    for load in load_state:
        load.wait()

    def adam_rows(n, carry):
        at = pl.ds(pl.multiple_of(n * 16, 16), 16)
        gradient = total[at, :] * SCALING
        first_new = beta_one * one[at, :].astype(F32) + (1.0 - beta_one) * gradient
        second_new = beta_two * two[at, :].astype(F32) + (1.0 - beta_two) * gradient * gradient
        step_size = first_new / bias_one / (jnp.sqrt(second_new / bias_two) + epsilon)
        old = master[at, :]
        new = old - learn_rate * (step_size + weight_decay * old)
        master[at, :] = new
        one[at, :] = first_new.astype(BF16)
        two[at, :] = second_new.astype(BF16)
        low = new.astype(BF16)
        fresh[r, at, :] = low
        for s in range(SEVEN):
            strips[s, at, :] = low[:, s * UNIT : (s + 1) * UNIT]
        return carry

    lax.fori_loop(0, ROWS // 16, adam_rows, 0)

    def fresh_view(chunk, low, count):
        return fresh.at[chunk, pl.ds(low, count), :]

    ftree = Tree(fresh_view, place.rep_ids, place.rep_dev, fresh_s, fresh_r, ROWS, 384)

    def strip_of(device):
        return pl.ds(pl.multiple_of(device * STRIP, STRIP), STRIP)

    def one_to(k):
        to = (t + k) % TP
        return remote(strips.at[:, strip_of(to), :], strewn.at[pl.ds(t * SEVEN, SEVEN)], p1_s, p1_r, k, (r, to))

    def one_from(k):
        source = (t + TP - k) % TP
        ref = strewn.at[pl.ds(source * SEVEN, SEVEN)]
        return remote(ref, ref, p1_s, p1_r, k, (r, source))

    each(TP, lambda k: one_to(k).start())
    ftree.begin()
    strewn[pl.ds(t * SEVEN, SEVEN)] = strips[:, strip_of(t), :]
    stores = []

    def storing(source, target):
        copy = pltpu.make_async_copy(source, target, outs.at[len(stores)])
        copy.start()
        stores.append(copy)

    storing(master, master_out)
    storing(one, one_out)
    storing(two, two_out)
    storing(fresh.at[r], full_out.at[r])

    load_maps.wait()
    narrow, rank, count = [], [], jnp.int32(0)
    for q in range(REP):
        narrow.append(maps[q, 0, 0] != -1)
        rank.append(jnp.minimum(count, KINDS - 1))
        count = count + jnp.where(narrow[q], 1, 0)
    which = []
    for k in range(KINDS):
        chosen = jnp.int32(0)
        for q in range(REP):
            chosen = jnp.where(narrow[q] & (rank[q] == k), q, chosen)
        which.append(chosen)

    each(TP, lambda k: one_from(k).wait_recv())
    for k in range(KINDS):

        def pick(to, carry, k=k):
            piece = maps[which[k], 0, to]
            value = strewn[jnp.maximum(piece, 0)]
            picked[to, k] = jnp.where(piece >= 0, value, jnp.zeros_like(value))
            return carry

        lax.fori_loop(0, TP, pick, 0)

    def two_to(k):
        to = (t + k) % TP
        return remote(picked.at[to], routed.at[:, strip_of(t), :], p2_s, p2_r, k, (r, to))

    def two_from(k):
        source = (t + TP - k) % TP
        ref = routed.at[:, strip_of(source), :]
        return remote(ref, ref, p2_s, p2_r, k, (r, source))

    each(TP, lambda k: two_to(k).start())
    routed[:, strip_of(t), :] = picked[t]

    def stored(name):
        chunk = ftree.names[name]
        storing(fresh.at[chunk], full_out.at[chunk])

    fsteps = ftree.steps(stored)
    for step in fsteps[:1]:
        step()
    each(TP, lambda k: two_from(k).wait_recv())
    for q in range(REP):
        value = routed[rank[q]]
        outgoing[q] = jnp.where(narrow[q], value, jnp.zeros_like(value))

    def three_to(k):
        to = (r + k) % REP
        return remote(outgoing.at[to], adopted.at[r], p3_s, p3_r, k, (to, t))

    def three_from(k):
        source = (r + REP - k) % REP
        return remote(adopted.at[source], adopted.at[source], p3_s, p3_r, k, (source, t))

    each(REP, lambda k: three_to(k).start())
    adopted[r] = outgoing[r]
    for step in fsteps[1:]:
        step()
    each(REP, lambda k: three_from(k).wait_recv())
    storing(adopted, adopted_out)

    for book in (tree, sibs, tree2, sibs2, ptree, sibs3, gtree, ftree):
        book.drain()
    each(REP, lambda k: map_to(k).wait_send())
    each(TP, lambda k: share_to(k).wait_send())
    each(REP, lambda k: swap_to(k).wait_send())
    each(TP, lambda k: one_to(k).wait_send())
    each(TP, lambda k: two_to(k).wait_send())
    each(REP, lambda k: three_to(k).wait_send())
    for store in stores:
        store.wait()


ANY = pl.BlockSpec(memory_space=pl.ANY)
VM = pl.BlockSpec(memory_space=pltpu.VMEM)
SM = pl.BlockSpec(memory_space=pltpu.SMEM)


def sems(*counts):
    return [pltpu.SemaphoreType.DMA((n,)) for n in counts for _ in (0, 1)]


def on_device(
    batch_rows, token_slots, holder_map, copies, upstream, up_act, master, moment1, moment2
):
    own_entry = jnp.sum(jnp.where(jnp.arange(TP) == lax.axis_index("tp"), holder_map[0], 0))
    master_next, one_next, two_next, full, adopted, _ = pl.pallas_call(
        step_kernel,
        out_shape=(
            jax.ShapeDtypeStruct((ROWS, WIDE), F32),
            jax.ShapeDtypeStruct((ROWS, WIDE), BF16),
            jax.ShapeDtypeStruct((ROWS, WIDE), BF16),
            jax.ShapeDtypeStruct((REP, ROWS, WIDE), BF16),
            jax.ShapeDtypeStruct((REP, ROWS, UNIT), BF16),
            jax.ShapeDtypeStruct((REP, 1, TP), jnp.int32),
        ),
        in_specs=[ANY, VM, SM, ANY, ANY, ANY, ANY, ANY, ANY, ANY],
        out_specs=(ANY,) * 6,
        scratch_shapes=[
            pltpu.VMEM((OWN, D), BF16),
            pltpu.VMEM((TP * OWN, SHARE), BF16),
            pltpu.VMEM((TP, TOK, SHARE), BF16),
            pltpu.VMEM((D, NARROW), BF16),
            pltpu.VMEM((TOK, NARROW), F32),
            pltpu.VMEM((TOK, NARROW), BF16),
            pltpu.VMEM((TOK, NARROW), BF16),
            pltpu.VMEM((TOK, NARROW), BF16),
            pltpu.VMEM((TP, TOK, UNIT), BF16),
            pltpu.VMEM((REP, TOK, ROWS), BF16),
            pltpu.VMEM((REP, TOK, WIDE), BF16),
            pltpu.VMEM((ROWS, WIDE), F32),
            pltpu.VMEM((REP, ROWS, WIDE), BF16),
            pltpu.VMEM((SEVEN, ROWS, UNIT), BF16),
            pltpu.VMEM((TP * SEVEN, STRIP, UNIT), BF16),
            pltpu.VMEM((TP, KINDS, STRIP, UNIT), BF16),
            pltpu.VMEM((KINDS, ROWS, UNIT), BF16),
            pltpu.VMEM((REP, ROWS, UNIT), BF16),
            pltpu.VMEM((REP, ROWS, UNIT), BF16),
            pltpu.VMEM((ROWS, WIDE), F32),
            pltpu.VMEM((ROWS, WIDE), BF16),
            pltpu.VMEM((ROWS, WIDE), BF16),
            pltpu.SMEM((REP, 1, TP), jnp.int32),
            *sems(REP, TP, 13, 8, 13, 8),
            *sems(REP, 13, 8, 13, 13, TP, TP, REP),
            pltpu.SemaphoreType.DMA((11,)),
            pltpu.SemaphoreType.DMA((12,)),
        ],
        compiler_params=pltpu.CompilerParams(
            collective_id=0, has_side_effects=True, vmem_limit_bytes=60 << 20
        ),
        name="step",
    )(
        batch_rows, token_slots.reshape(TOK, 1), holder_map, holder_map, copies, upstream, up_act,
        master, moment1, moment2,
    )
    copy_next = jnp.concatenate([full.reshape(D, WIDE), adopted.reshape(D, UNIT)], axis=1)
    copy_next = jnp.where(own_entry == -2, jnp.zeros_like(copy_next), copy_next)
    return master_next, one_next, two_next, copy_next


def solution(mesh):
    placed = (
        P(("rep", "tp"), None),
        P("rep", None),
        P("rep", None),
        P("rep", "tp"),
        P("rep", "tp"),
        P("rep", "tp"),
        P("rep", "tp"),
        P("rep", "tp"),
        P("rep", "tp"),
    )
    return jax.shard_map(
        on_device,
        mesh=mesh,
        in_specs=placed,
        out_specs=(P("rep", "tp"), P("rep", "tp"), P("rep", "tp"), P("rep", "tp")),
        check_vma=False,
    )
```

time: 223 us -> 212 us (0.951)
  Pallas kernels: 207 us -> 196 us
    pallas_call x2 -> x1, Pallas kernels: 207 us -> 196 us  [on_device(): pl.pallas_call(step_kernel, out_shape=(jax.ShapeDtypeStruct((ROWS, WIDE),...]
where the time goes in v3:
time: 212 us; the launch traced here: 211 us
  Pallas kernels  196 us (92%)
  other arithmetic  9.24 us (4%)
  local copies, waits for them, and re-layouts  4.59 us (2%)
    pallas_call x1, Pallas kernels, on_device(): pl.pallas_call(step_kernel, out_shape=(jax.ShapeDtypeStruct((ROWS, WIDE),...  196 us
    select_n x1, other arithmetic, on_device(): copy_next = jnp.where(own_entry == -2, jnp.zeros_like(copy_next), copy_next)  7.94 us

profile of v3, /device:TPU:0, one launch (start us, length us, event | category | flops | bytes accessed | tf_op | source)
XLA Modules:
  0.0 211.4 jit_solution(12760150795958410320)
XLA Ops:
  0.6 1.3 fusion
  2.6 1.5 copy.13.slots_ref
  4.1 196.3 %step.1 = (f32[512,896]{1,0:T(8,128)}, bf16[512,896]{1,0:T(8,128)(2,1)}, bf16[512,896]{1,0:T(8,128)(2,1)}, bf16[8,512,896]{2,1,0:T(8,128)(2,1)}, bf16[8,512,128]{2,1,0:T(8,128)(2,1)}, /*index=5*/s32[8,1,16]{2,1,0:T(1,128)}) custom-call(bf16[96,4096]{1,0:T(8,128)(2,1)} %rows_ref.1, s32[384,1]{1,0:T(8,128)} %copy.13.slots_ref, s32[1,16]{1,0:T(1,128)} %map_ref.1, ...), custom_call_target="tpu_custom_call" | custom-call | tf_op jit(solution)/shard_map/step/pallas_call | solution.py:535
  200.4 0.0 copy-start
  200.4 0.0 copy-start.2
  200.4 0.0 copy-start.1
  200.4 7.9 %maximum_select_fusion = bf16[4096,1024]{1,0:T(8,128)(2,1)} fusion(bf16[4096,128]{1,0:T(8,128)(2,1)} %bitcast.6, bf16[4096,896]{1,0:T(8,128)(2,1)} %bitcast.5, pred[]{:T(512)S(6)} %eq.11), kind=kLoop, calls=%fused_computation | loop fusion | flops 20971520 | bytes 16777216 | tf_op jit(solution)/shard_map/jit(_where)/select_n | solution.py:585
  208.4 0.0 copy-done
  208.4 1.2 copy.17
  209.6 0.0 copy-done.2
  209.6 0.9 copy.18
  210.5 0.0 copy-done.1
  210.5 0.9 copy.19
Async XLA Ops:
  200.4 8.0 %copy-start = (f32[512,896]{1,0:T(8,128)S(1)}, f32[512,896]{1,0:T(8,128)}, u32[]{:S(2)}) copy-start(f32[512,896]{1,0:T(8,128)} %get-tuple-element.18) | copy-start | bytes 5505028
  200.4 9.2 %copy-start.2 = (bf16[512,896]{1,0:T(8,128)(2,1)S(1)}, bf16[512,896]{1,0:T(8,128)(2,1)}, u32[]{:S(2)}) copy-start(bf16[512,896]{1,0:T(8,128)(2,1)} %get-tuple-element.19) | copy-start | bytes 2752516
  200.4 10.1 %copy-start.1 = (bf16[512,896]{1,0:T(8,128)(2,1)S(1)}, bf16[512,896]{1,0:T(8,128)(2,1)}, u32[]{:S(2)}) copy-start(bf16[512,896]{1,0:T(8,128)(2,1)} %get-tuple-element.20) | copy-start | bytes 2752516

commit v4 on v3

--- a/solution.py
+++ b/solution.py
@@ -191,7 +191,7 @@
 def step_kernel(
     rows_ref, slots_ref, holders_ref, map_ref, copies_ref, upstream_ref, act_ref, master_ref, one_ref, two_ref,
     master_out, one_out, two_out, full_out, adopted_out, maps_out,
-    own_rows, spread, inputs, weight, gates, upstream, act, grad, pieces,
+    own_rows, spread, inputs, choice, weight, gates, upstream, act, grad, pieces,
     parts, grads, total, fresh, strips, strewn, picked, routed, outgoing, adopted, master, one, two, maps,
     map_s, map_r, row_s, row_r, tree_s, tree_r, sib_s, sib_r, tree2_s, tree2_r, sib2_s, sib2_r,
     swap_s, swap_r, part_s, part_r, sib3_s, sib3_r, grad_s, grad_r, fresh_s, fresh_r,
@@ -221,6 +221,9 @@
             src_ref=source, dst_ref=target, send_sem=s.at[k], recv_sem=r_.at[k], device_id=to, device_id_type=MESH
         )
 
+    def columns_of(device):
+        return pl.ds(pl.multiple_of(device * SHARE, SHARE), SHARE)
+
     def share_to(k):
         to = (t + k) % TP
         return remote(
@@ -247,20 +250,20 @@
         return remote(map_ref, maps_out.at[source], map_s, map_r, k, (source, t))
 
     each(REP, lambda k: map_to(k).start())
+    def choose(n, carry):
+        at = pl.ds(pl.multiple_of(n * 16, 16), 16)
+        places = lax.broadcasted_iota(jnp.int32, (16, TP * OWN), 1)
+        choice[at, :] = jnp.where(slots_ref[at, :] == places, 1.0, 0.0).astype(BF16)
+        return carry
+
+    lax.fori_loop(0, TOK // 16, choose, 0)
     own_share.wait()
     each(TP, lambda k: share_from(k).wait_recv())
 
-    slots = slots_ref[...]
-    found = jnp.zeros((TOK, SHARE), F32)
-    block = 512
-    for b in range(TP * OWN // block):
-        places = lax.broadcasted_iota(jnp.int32, (TOK, block), 1) + b * block
-        one_hot = jnp.where(slots == places, 1.0, 0.0).astype(BF16)
-        found += jnp.dot(one_hot, spread[b * block : (b + 1) * block, :], preferred_element_type=F32)
-    inputs[t] = found.astype(BF16)
+    inputs[:, columns_of(t)] = jnp.dot(choice[...], spread[...], preferred_element_type=F32).astype(BF16)
 
     def input_view(chunk, low, count):
-        return inputs.at[chunk, pl.ds(low, count), :]
+        return inputs.at[pl.ds(low, count), columns_of(chunk)]
 
     tree = Tree(input_view, place.tp_ids, place.tp_dev, tree_s, tree_r, TOK, 224)
     sibs = Siblings(tree, input_view, TOK, place, sib_s, sib_r)
@@ -268,31 +271,27 @@
     sibs.start("me")
     load_weight.wait()
 
-    def multiplied(chunk, first=False):
-        depth = pl.ds(pl.multiple_of(chunk * SHARE, SHARE), SHARE)
-        for n in range(4):
-            cols = slice(n * 256, (n + 1) * 256)
-            part = jnp.dot(inputs[chunk], weight[depth, cols], preferred_element_type=F32)
+    def multiplied(name, first=False):
+        sibs.wait(name)
+        depth = pl.ds(pl.multiple_of(tree.names[name] // 2 * (2 * SHARE), 2 * SHARE), 2 * SHARE)
+        for n in range(2):
+            cols = slice(n * 512, (n + 1) * 512)
+            part = jnp.dot(inputs[:, depth], weight[depth, cols], preferred_element_type=F32)
             gates[:, cols] = part if first else gates[:, cols] + part
 
-    def other_multiplied(name):
-        sibs.wait(name)
-        multiplied(tree.names[name] + 1 - 2 * place.core)
-
-    multiplied(t, True)
     waiting = ["me"]
 
     def whole(name):
         sibs.start(name)
-        multiplied(tree.names[name])
         waiting.append(name)
         if len(waiting) > 2:
-            other_multiplied(waiting.pop(0))
+            before = waiting.pop(0)
+            multiplied(before, before == "me")
 
     for step in tree.steps(whole):
         step()
     for name in waiting:
-        other_multiplied(name)
+        multiplied(name)
 
     mine_rows = pl.ds(pl.multiple_of(place.chip * PART, PART), PART)
     mine_cols = pl.ds(pl.multiple_of(place.core * SHARE, SHARE), SHARE)
@@ -300,7 +299,7 @@
     def swap_to(k):
         to = (r + k) % REP
         return remote(
-            inputs.at[2 * to + place.core, mine_rows, :], parts.at[r, mine_rows, mine_cols], swap_s, swap_r, k, (to, t)
+            inputs.at[mine_rows, columns_of(2 * to + place.core)], parts.at[r, mine_rows, mine_cols], swap_s, swap_r, k, (to, t)
         )
 
     def swap_from(k):
@@ -309,22 +308,29 @@
         return remote(ref, ref, swap_s, swap_r, k, (source, t))
 
     each(REP, lambda k: swap_to(k).start())
-    own_swap = loading(9, inputs.at[2 * r + place.core, mine_rows, :], parts.at[r, mine_rows, mine_cols])
+    own_swap = loading(9, inputs.at[mine_rows, columns_of(2 * r + place.core)], parts.at[r, mine_rows, mine_cols])
 
     for load in load_factors:
         load.wait()
 
-    def gate_rows(n, carry):
-        at = pl.ds(pl.multiple_of(n * 16, 16), 16)
-        gate = gates[at, :] * SCALING
-        logistic = 1.0 / (1.0 + jnp.exp(-gate))
-        grad[at, :] = (
-            upstream[at, :].astype(F32) * act[at, :].astype(F32) * logistic * (1.0 + gate * (1.0 - logistic))
-        ).astype(BF16)
-        return carry
-
-    lax.fori_loop(0, TOK // 16, gate_rows, 0)
-    pieces[t] = grad[:, WIDE:]
+    def gate_rows(tall, cols, keep):
+        def rows(n, carry):
+            at = pl.ds(pl.multiple_of(n * tall, tall), tall)
+            gate = gates[at, cols] * SCALING
+            logistic = 1.0 / (1.0 + jnp.exp(-gate))
+            factors = upstream[at, cols].astype(F32) * act[at, cols].astype(F32)
+            keep(at, (factors * logistic * (1.0 + gate * (1.0 - logistic))).astype(BF16))
+            return carry
+
+        lax.fori_loop(0, TOK // tall, rows, 0)
+
+    def keep_piece(at, value):
+        pieces[t, at, :] = value
+
+    def keep_wide(at, value):
+        grad[at, :] = value
+
+    gate_rows(64, slice(WIDE, NARROW), keep_piece)
 
     def piece_view(chunk, low, count):
         return pieces.at[chunk, pl.ds(low, count), :]
@@ -333,10 +339,27 @@
     sibs2 = Siblings(tree2, piece_view, TOK, place, sib2_s, sib2_r)
     tree2.begin()
     sibs2.start("me")
-    for step in tree2.steps(sibs2.start):
+    gate_rows(16, slice(0, WIDE), keep_wide)
+
+    def part_view(chunk, low, count):
+        at, side = chunk // 2, chunk % 2
+        return parts.at[
+            pl.ds(low, count),
+            pl.ds(pl.multiple_of(at * PART, PART), PART),
+            pl.ds(pl.multiple_of(side * SHARE, SHARE), SHARE),
+        ]
+
+    ptree = Tree(part_view, place.tp_ids, place.tp_dev, part_s, part_r, REP, REP)
+    sibs3 = Siblings(ptree, part_view, REP, place, sib3_s, sib3_r)
+    steps2 = tree2.steps(sibs2.start)
+    for step in steps2[:5]:
         step()
     own_swap.wait()
     each(REP, lambda k: swap_from(k).wait_recv())
+    ptree.begin()
+    sibs3.start("me")
+    for step in steps2[5:]:
+        step()
     for name in ORDER:
         sibs2.wait(name)
 
@@ -352,21 +375,8 @@
     def grad_view(chunk, low, count):
         return grads.at[chunk, pl.ds(low, count), :]
 
-    gtree = Tree(grad_view, place.rep_ids, place.rep_dev, grad_s, grad_r, TOK, 224)
+    gtree = Tree(grad_view, place.rep_ids, place.rep_dev, grad_s, grad_r, TOK, 256)
     gtree.begin()
-
-    def part_view(chunk, low, count):
-        at, side = chunk // 2, chunk % 2
-        return parts.at[
-            pl.ds(low, count),
-            pl.ds(pl.multiple_of(at * PART, PART), PART),
-            pl.ds(pl.multiple_of(side * SHARE, SHARE), SHARE),
-        ]
-
-    ptree = Tree(part_view, place.tp_ids, place.tp_dev, part_s, part_r, REP, REP)
-    sibs3 = Siblings(ptree, part_view, REP, place, sib3_s, sib3_r)
-    ptree.begin()
-    sibs3.start("me")
 
     def gathered(chunk, first=False):
         part = lax.dot_general(
@@ -378,12 +388,9 @@
     each(REP, lambda k: map_from(k).wait_recv())
     load_maps = loading(10, maps_out, maps)
     gsteps = gtree.steps(lambda name: gathered(gtree.names[name]))
-    psteps = ptree.steps(sibs3.start)
-    for step in psteps[:5]:
+    for step in ptree.steps(sibs3.start):
         step()
     gsteps[0]()
-    for step in psteps[5:]:
-        step()
     for name in ORDER:
         sibs3.wait(name)
     gathered(r, True)
@@ -392,6 +399,13 @@
 
     for load in load_state:
         load.wait()
+
+    def strip_of(device):
+        return pl.ds(pl.multiple_of(device * STRIP, STRIP), STRIP)
+
+    def one_to(k):
+        to = (t + k) % TP
+        return remote(strips.at[:, strip_of(to), :], strewn.at[pl.ds(t * SEVEN, SEVEN)], p1_s, p1_r, k, (r, to))
 
     def adam_rows(n, carry):
         at = pl.ds(pl.multiple_of(n * 16, 16), 16)
@@ -410,26 +424,28 @@
             strips[s, at, :] = low[:, s * UNIT : (s + 1) * UNIT]
         return carry
 
-    lax.fori_loop(0, ROWS // 16, adam_rows, 0)
+    def strip_done(k, carry):
+        to = (t + 1 + k) % TP
+        lax.fori_loop(2 * to, 2 * to + 2, adam_rows, 0)
+
+        @pl.when(k < TP - 1)
+        def _():
+            one_to(k + 1).start()
+
+        return carry
+
+    lax.fori_loop(0, TP, strip_done, 0)
 
     def fresh_view(chunk, low, count):
         return fresh.at[chunk, pl.ds(low, count), :]
 
-    ftree = Tree(fresh_view, place.rep_ids, place.rep_dev, fresh_s, fresh_r, ROWS, 384)
-
-    def strip_of(device):
-        return pl.ds(pl.multiple_of(device * STRIP, STRIP), STRIP)
-
-    def one_to(k):
-        to = (t + k) % TP
-        return remote(strips.at[:, strip_of(to), :], strewn.at[pl.ds(t * SEVEN, SEVEN)], p1_s, p1_r, k, (r, to))
+    ftree = Tree(fresh_view, place.rep_ids, place.rep_dev, fresh_s, fresh_r, ROWS, 320)
 
     def one_from(k):
         source = (t + TP - k) % TP
         ref = strewn.at[pl.ds(source * SEVEN, SEVEN)]
         return remote(ref, ref, p1_s, p1_r, k, (r, source))
 
-    each(TP, lambda k: one_to(k).start())
     ftree.begin()
     strewn[pl.ds(t * SEVEN, SEVEN)] = strips[:, strip_of(t), :]
     stores = []
@@ -485,7 +501,7 @@
         storing(fresh.at[chunk], full_out.at[chunk])
 
     fsteps = ftree.steps(stored)
-    for step in fsteps[:1]:
+    for step in fsteps[:3]:
         step()
     each(TP, lambda k: two_from(k).wait_recv())
     for q in range(REP):
@@ -502,7 +518,7 @@
 
     each(REP, lambda k: three_to(k).start())
     adopted[r] = outgoing[r]
-    for step in fsteps[1:]:
+    for step in fsteps[3:]:
         step()
     each(REP, lambda k: three_from(k).wait_recv())
     storing(adopted, adopted_out)
@@ -547,12 +563,13 @@
         scratch_shapes=[
             pltpu.VMEM((OWN, D), BF16),
             pltpu.VMEM((TP * OWN, SHARE), BF16),
-            pltpu.VMEM((TP, TOK, SHARE), BF16),
+            pltpu.VMEM((TOK, D), BF16),
+            pltpu.VMEM((TOK, TP * OWN), BF16),
             pltpu.VMEM((D, NARROW), BF16),
             pltpu.VMEM((TOK, NARROW), F32),
             pltpu.VMEM((TOK, NARROW), BF16),
             pltpu.VMEM((TOK, NARROW), BF16),
-            pltpu.VMEM((TOK, NARROW), BF16),
+            pltpu.VMEM((TOK, WIDE), BF16),
             pltpu.VMEM((TP, TOK, UNIT), BF16),
             pltpu.VMEM((REP, TOK, ROWS), BF16),
             pltpu.VMEM((REP, TOK, WIDE), BF16),

time: 212 us -> 190 us (0.90)
  Pallas kernels: 196 us -> 174 us
    pallas_call x1, Pallas kernels: 196 us -> 174 us  [on_device(): pl.pallas_call(step_kernel, out_shape=(jax.ShapeDtypeStruct((ROWS, WIDE),...]
where the time goes in v4:
time: 190 us; the launch traced here: 189 us
  Pallas kernels  174 us (92%)
  other arithmetic  9.24 us (5%)
  local copies, waits for them, and re-layouts  4.59 us (2%)
    pallas_call x1, Pallas kernels, on_device(): pl.pallas_call(step_kernel, out_shape=(jax.ShapeDtypeStruct((ROWS, WIDE),...  174 us
    select_n x1, other arithmetic, on_device(): copy_next = jnp.where(own_entry == -2, jnp.zeros_like(copy_next), copy_next)  7.94 us

profile of v4, /device:TPU:0, one launch (start us, length us, event | category | flops | bytes accessed | tf_op | source)
XLA Modules:
  0.0 189.3 jit_solution(70401096301393609)
XLA Ops:
  0.6 1.3 fusion
  2.6 1.5 copy.13.slots_ref
  4.1 174.1 %step.1 = (f32[512,896]{1,0:T(8,128)}, bf16[512,896]{1,0:T(8,128)(2,1)}, bf16[512,896]{1,0:T(8,128)(2,1)}, bf16[8,512,896]{2,1,0:T(8,128)(2,1)}, bf16[8,512,128]{2,1,0:T(8,128)(2,1)}, /*index=5*/s32[8,1,16]{2,1,0:T(1,128)}) custom-call(bf16[96,4096]{1,0:T(8,128)(2,1)} %rows_ref.1, s32[384,1]{1,0:T(8,128)} %copy.13.slots_ref, s32[1,16]{1,0:T(1,128)} %map_ref.1, ...), custom_call_target="tpu_custom_call" | custom-call | tf_op jit(solution)/shard_map/step/pallas_call | solution.py:551
  178.2 0.0 copy-start
  178.2 0.0 copy-start.2
  178.3 0.0 copy-start.1
  178.3 7.9 %maximum_select_fusion = bf16[4096,1024]{1,0:T(8,128)(2,1)} fusion(bf16[4096,128]{1,0:T(8,128)(2,1)} %bitcast.6, bf16[4096,896]{1,0:T(8,128)(2,1)} %bitcast.5, pred[]{:T(512)S(6)} %eq.11), kind=kLoop, calls=%fused_computation | loop fusion | flops 20971520 | bytes 16777216 | tf_op jit(solution)/shard_map/jit(_where)/select_n | solution.py:602
  186.2 0.0 copy-done
  186.2 1.2 copy.17
  187.4 0.0 copy-done.2
  187.4 0.9 copy.18
  188.4 0.0 copy-done.1
  188.4 0.9 copy.19
Async XLA Ops:
  178.2 8.0 %copy-start = (f32[512,896]{1,0:T(8,128)S(1)}, f32[512,896]{1,0:T(8,128)}, u32[]{:S(2)}) copy-start(f32[512,896]{1,0:T(8,128)} %get-tuple-element.18) | copy-start | bytes 5505028
  178.2 9.2 %copy-start.2 = (bf16[512,896]{1,0:T(8,128)(2,1)S(1)}, bf16[512,896]{1,0:T(8,128)(2,1)}, u32[]{:S(2)}) copy-start(bf16[512,896]{1,0:T(8,128)(2,1)} %get-tuple-element.19) | copy-start | bytes 2752516
  178.3 10.1 %copy-start.1 = (bf16[512,896]{1,0:T(8,128)(2,1)S(1)}, bf16[512,896]{1,0:T(8,128)(2,1)}, u32[]{:S(2)}) copy-start(bf16[512,896]{1,0:T(8,128)(2,1)} %get-tuple-element.20) | copy-start | bytes 2752516

commit v5 on v4

--- a/solution.py
+++ b/solution.py
@@ -24,6 +24,7 @@
 SEVEN = WIDE // UNIT
 PART = TOK // (TP // 2)
 KINDS = REP // 2
+LIMIT = 50
 SCALING = 1.0 / math.sqrt(D)
 MESH = pl.DeviceIdType.MESH
 F32, BF16 = jnp.float32, jnp.bfloat16
@@ -190,12 +191,12 @@
 
 def step_kernel(
     rows_ref, slots_ref, holders_ref, map_ref, copies_ref, upstream_ref, act_ref, master_ref, one_ref, two_ref,
-    master_out, one_out, two_out, full_out, adopted_out, maps_out,
-    own_rows, spread, inputs, choice, weight, gates, upstream, act, grad, pieces,
-    parts, grads, total, fresh, strips, strewn, picked, routed, outgoing, adopted, master, one, two, maps,
+    master, one, two, fresh, adopted, maps_out,
+    own_rows, spread, inputs, column, choice, weight, gates, upstream, act, grad, pieces,
+    parts, grads, total, strips, strewn, picked, routed, outgoing, maps,
     map_s, map_r, row_s, row_r, tree_s, tree_r, sib_s, sib_r, tree2_s, tree2_r, sib2_s, sib2_r,
     swap_s, swap_r, part_s, part_r, sib3_s, sib3_r, grad_s, grad_r, fresh_s, fresh_r,
-    p1_s, p1_r, p2_s, p2_r, p3_s, p3_r, local, outs,
+    p1_s, p1_r, p2_s, p2_r, p3_s, p3_r, local,
 ):
     place = Place()
     r, t = place.r, place.t
@@ -250,10 +251,12 @@
         return remote(map_ref, maps_out.at[source], map_s, map_r, k, (source, t))
 
     each(REP, lambda k: map_to(k).start())
+    column[...] = jnp.broadcast_to(slots_ref[...], (128, TOK)).T
+
     def choose(n, carry):
         at = pl.ds(pl.multiple_of(n * 16, 16), 16)
         places = lax.broadcasted_iota(jnp.int32, (16, TP * OWN), 1)
-        choice[at, :] = jnp.where(slots_ref[at, :] == places, 1.0, 0.0).astype(BF16)
+        choice[at, :] = jnp.where(column[at, :1] == places, 1.0, 0.0).astype(BF16)
         return carry
 
     lax.fori_loop(0, TOK // 16, choose, 0)
@@ -448,17 +451,6 @@
 
     ftree.begin()
     strewn[pl.ds(t * SEVEN, SEVEN)] = strips[:, strip_of(t), :]
-    stores = []
-
-    def storing(source, target):
-        copy = pltpu.make_async_copy(source, target, outs.at[len(stores)])
-        copy.start()
-        stores.append(copy)
-
-    storing(master, master_out)
-    storing(one, one_out)
-    storing(two, two_out)
-    storing(fresh.at[r], full_out.at[r])
 
     load_maps.wait()
     narrow, rank, count = [], [], jnp.int32(0)
@@ -496,11 +488,7 @@
     each(TP, lambda k: two_to(k).start())
     routed[:, strip_of(t), :] = picked[t]
 
-    def stored(name):
-        chunk = ftree.names[name]
-        storing(fresh.at[chunk], full_out.at[chunk])
-
-    fsteps = ftree.steps(stored)
+    fsteps = ftree.steps(lambda name: None)
     for step in fsteps[:3]:
         step()
     each(TP, lambda k: two_from(k).wait_recv())
@@ -521,7 +509,6 @@
     for step in fsteps[3:]:
         step()
     each(REP, lambda k: three_from(k).wait_recv())
-    storing(adopted, adopted_out)
 
     for book in (tree, sibs, tree2, sibs2, ptree, sibs3, gtree, ftree):
         book.drain()
@@ -531,6 +518,35 @@
     each(TP, lambda k: one_to(k).wait_send())
     each(TP, lambda k: two_to(k).wait_send())
     each(REP, lambda k: three_to(k).wait_send())
+
+
+def finish_kernel(
+    holders_ref, master, one, two, fresh, adopted, master_out, one_out, two_out, copy_out, stage, outs
+):
+    failed = holders_ref[0, lax.axis_index("tp")] == -2
+    stores = []
+
+    def storing(source, target):
+        copy = pltpu.make_async_copy(source, target, outs.at[len(stores)])
+        copy.start()
+        stores.append(copy)
+
+    storing(master, master_out)
+    storing(one, one_out)
+    storing(two, two_out)
+    for chunk in range(REP):
+
+        def rows(n, carry, chunk=chunk):
+            at = pl.ds(pl.multiple_of(n * 32, 32), 32)
+            to = pl.ds(pl.multiple_of(chunk * ROWS + n * 32, 32), 32)
+            for source, cols in ((fresh, slice(0, WIDE)), (adopted, slice(WIDE, NARROW))):
+                value = source[chunk, at, :]
+                stage[to, cols] = jnp.where(failed, jnp.zeros_like(value), value)
+            return carry
+
+        lax.fori_loop(0, ROWS // 32, rows, 0)
+        span = pl.ds(chunk * ROWS, ROWS)
+        storing(stage.at[span], copy_out.at[span])
     for store in stores:
         store.wait()
 
@@ -547,23 +563,26 @@
 def on_device(
     batch_rows, token_slots, holder_map, copies, upstream, up_act, master, moment1, moment2
 ):
-    own_entry = jnp.sum(jnp.where(jnp.arange(TP) == lax.axis_index("tp"), holder_map[0], 0))
-    master_next, one_next, two_next, full, adopted, _ = pl.pallas_call(
+    state = (
+        jax.ShapeDtypeStruct((ROWS, WIDE), F32),
+        jax.ShapeDtypeStruct((ROWS, WIDE), BF16),
+        jax.ShapeDtypeStruct((ROWS, WIDE), BF16),
+    )
+    *held, _ = pl.pallas_call(
         step_kernel,
         out_shape=(
-            jax.ShapeDtypeStruct((ROWS, WIDE), F32),
-            jax.ShapeDtypeStruct((ROWS, WIDE), BF16),
-            jax.ShapeDtypeStruct((ROWS, WIDE), BF16),
-            jax.ShapeDtypeStruct((REP, ROWS, WIDE), BF16),
-            jax.ShapeDtypeStruct((REP, ROWS, UNIT), BF16),
+            *(pltpu.VMEM(a.shape, a.dtype) for a in state),
+            pltpu.VMEM((REP, ROWS, WIDE), BF16),
+            pltpu.VMEM((REP, ROWS, UNIT), BF16),
             jax.ShapeDtypeStruct((REP, 1, TP), jnp.int32),
         ),
         in_specs=[ANY, VM, SM, ANY, ANY, ANY, ANY, ANY, ANY, ANY],
-        out_specs=(ANY,) * 6,
+        out_specs=(VM, VM, VM, VM, VM, ANY),
         scratch_shapes=[
             pltpu.VMEM((OWN, D), BF16),
             pltpu.VMEM((TP * OWN, SHARE), BF16),
             pltpu.VMEM((TOK, D), BF16),
+            pltpu.VMEM((TOK, 128), jnp.int32),
             pltpu.VMEM((TOK, TP * OWN), BF16),
             pltpu.VMEM((D, NARROW), BF16),
             pltpu.VMEM((TOK, NARROW), F32),
@@ -574,33 +593,33 @@
             pltpu.VMEM((REP, TOK, ROWS), BF16),
             pltpu.VMEM((REP, TOK, WIDE), BF16),
             pltpu.VMEM((ROWS, WIDE), F32),
-            pltpu.VMEM((REP, ROWS, WIDE), BF16),
             pltpu.VMEM((SEVEN, ROWS, UNIT), BF16),
             pltpu.VMEM((TP * SEVEN, STRIP, UNIT), BF16),
             pltpu.VMEM((TP, KINDS, STRIP, UNIT), BF16),
             pltpu.VMEM((KINDS, ROWS, UNIT), BF16),
             pltpu.VMEM((REP, ROWS, UNIT), BF16),
-            pltpu.VMEM((REP, ROWS, UNIT), BF16),
-            pltpu.VMEM((ROWS, WIDE), F32),
-            pltpu.VMEM((ROWS, WIDE), BF16),
-            pltpu.VMEM((ROWS, WIDE), BF16),
             pltpu.SMEM((REP, 1, TP), jnp.int32),
             *sems(REP, TP, 13, 8, 13, 8),
             *sems(REP, 13, 8, 13, 13, TP, TP, REP),
             pltpu.SemaphoreType.DMA((11,)),
-            pltpu.SemaphoreType.DMA((12,)),
         ],
         compiler_params=pltpu.CompilerParams(
-            collective_id=0, has_side_effects=True, vmem_limit_bytes=60 << 20
+            collective_id=0, has_side_effects=True, vmem_limit_bytes=LIMIT << 20
         ),
         name="step",
     )(
-        batch_rows, token_slots.reshape(TOK, 1), holder_map, holder_map, copies, upstream, up_act,
+        batch_rows, token_slots, holder_map, holder_map, copies, upstream, up_act,
         master, moment1, moment2,
     )
-    copy_next = jnp.concatenate([full.reshape(D, WIDE), adopted.reshape(D, UNIT)], axis=1)
-    copy_next = jnp.where(own_entry == -2, jnp.zeros_like(copy_next), copy_next)
-    return master_next, one_next, two_next, copy_next
+    return pl.pallas_call(
+        finish_kernel,
+        out_shape=(*state, jax.ShapeDtypeStruct((D, NARROW), BF16)),
+        in_specs=[SM, VM, VM, VM, VM, VM],
+        out_specs=(ANY,) * 4,
+        scratch_shapes=[pltpu.VMEM((D, NARROW), BF16), pltpu.SemaphoreType.DMA((11,))],
+        compiler_params=pltpu.CompilerParams(vmem_limit_bytes=16 << 20),
+        name="finish",
+    )(holder_map, *held)
 
 
 def solution(mesh):

time: 190 us -> 180 us (0.947)
  other arithmetic: 9.24 us -> 0 us
  local copies, waits for them, and re-layouts: 4.59 us -> 0.01 us
  Pallas kernels: 174 us -> 178 us
    select_n x1 -> x0, other arithmetic: 7.94 us -> none  [on_device(): copy_next = jnp.where(own_entry == -2, jnp.zeros_like(copy_next), copy_next)]
    pallas_call x1 -> x2, Pallas kernels: 174 us -> 178 us  [the longest x1 173 us: on_device(): pl.pallas_call(step_kernel, out_shape=(*(pltpu.VMEM(a.shape, a.dtype) for...]
    unnamed x9 -> x2, local copies, waits for them, and re-layouts: 3.09 us -> 0.01 us
where the time goes in v5:
time: 180 us; the launch traced here: 179 us
  Pallas kernels  178 us (99%)
    pallas_call x1, Pallas kernels, on_device(): pl.pallas_call(step_kernel, out_shape=(*(pltpu.VMEM(a.shape, a.dtype) for...  173 us
    pallas_call x1, Pallas kernels, on_device(): pl.pallas_call(finish_kernel, out_shape=(*state, jax.ShapeDtypeStruct((D,...  5.05 us

profile of v5, /device:TPU:0, one launch (start us, length us, event | category | flops | bytes accessed | tf_op | source)
XLA Modules:
  0.0 178.9 jit_solution(16805801741051057623)
XLA Ops:
  0.6 0.0 copy-start
  0.6 173.2 %step.1 = (f32[512,896]{1,0:T(8,128)S(1)}, bf16[512,896]{1,0:T(8,128)(2,1)S(1)}, bf16[512,896]{1,0:T(8,128)(2,1)S(1)}, bf16[8,512,896]{2,1,0:T(8,128)(2,1)S(1)},...) custom-call(bf16[96,4096]{1,0:T(8,128)(2,1)} %rows_ref.1, s32[1,384]{1,0:T(1,128)} %slots_ref.1, ...), custom_call_target="tpu_custom_call" | custom-call | tf_op jit(solution)/shard_map/step/pallas_call | solution.py:571
  173.9 0.0 copy-done
  173.9 5.1 %finish.1 = (f32[512,896]{1,0:T(8,128)}, bf16[512,896]{1,0:T(8,128)(2,1)}, bf16[512,896]{1,0:T(8,128)(2,1)}, bf16[4096,1024]{1,0:T(8,128)(2,1)}) custom-call(s32[1,16]{1,0:T(1,128)S(1)} %copy-done, f32[512,896]{1,0:T(8,128)S(1)} %get-tuple-element.9.master, bf16[512,896]{1,0:T(8,128)(2,1)S(1)} %get-tuple-element.10.one, ...), custom_call_target="tpu_custom_call" | custom-call | tf_op jit(solution)/shard_map/finish/pallas_call | solution.py:614
Async XLA Ops:
  0.6 173.2 %copy-start = (s32[1,16]{1,0:T(1,128)S(1)}, s32[1,16]{1,0:T(1,128)}, u32[]{:S(2)}) copy-start(s32[1,16]{1,0:T(1,128)} %holders_ref.3) | copy-start | bytes 196

commit v6 on v5

--- a/solution.py
+++ b/solution.py
@@ -25,6 +25,7 @@
 PART = TOK // (TP // 2)
 KINDS = REP // 2
 LIMIT = 50
+HALF = TOK // 2
 SCALING = 1.0 / math.sqrt(D)
 MESH = pl.DeviceIdType.MESH
 F32, BF16 = jnp.float32, jnp.bfloat16
@@ -73,7 +74,7 @@
 
 
 class Tree:
-    def __init__(self, view, ids, dev, ssem, rsem, extent, first):
+    def __init__(self, view, ids, dev, ssem, rsem, extent, first, base=0):
         (me, nx, pv, op), (me_p, nx_p, pv_p, op_p) = ids
         to_nx, to_pv, to_pair = dev(nx), dev(pv), dev(me_p)
         half, a_half, rest = extent // 2, first // 2, extent - first
@@ -92,7 +93,7 @@
                 for book, which in ((self.out, chunk), (self.into, got[i])):
                     ref = view(which, low, count)
                     book[i] = pltpu.make_async_remote_copy(
-                        src_ref=ref, dst_ref=ref, send_sem=ssem.at[i - 1], recv_sem=rsem.at[i - 1],
+                        src_ref=ref, dst_ref=ref, send_sem=ssem.at[base + i - 1], recv_sem=rsem.at[base + i - 1],
                         device_id=to, device_id_type=MESH,
                     )
 
@@ -167,14 +168,14 @@
 
 
 class Siblings:
-    def __init__(self, tree, view, extent, place, ssem, rsem):
+    def __init__(self, tree, view, extent, place, ssem, rsem, base=0):
         self.out, self.into = {}, {}
         for n, name in enumerate(ORDER):
             mine = tree.names[name]
             for book, which in ((self.out, mine), (self.into, mine + 1 - 2 * place.core)):
                 ref = view(which, 0, extent)
                 book[name] = pltpu.make_async_remote_copy(
-                    src_ref=ref, dst_ref=ref, send_sem=ssem.at[n], recv_sem=rsem.at[n],
+                    src_ref=ref, dst_ref=ref, send_sem=ssem.at[base + n], recv_sem=rsem.at[base + n],
                     device_id=place.sibling, device_id_type=MESH,
                 )
 
@@ -192,7 +193,7 @@
 def step_kernel(
     rows_ref, slots_ref, holders_ref, map_ref, copies_ref, upstream_ref, act_ref, master_ref, one_ref, two_ref,
     master, one, two, fresh, adopted, maps_out,
-    own_rows, spread, inputs, column, choice, weight, gates, upstream, act, grad, pieces,
+    own_rows, spread, inputs, column, choice, weight, gates, upstream, act, grad, early, later,
     parts, grads, total, strips, strewn, picked, routed, outgoing, maps,
     map_s, map_r, row_s, row_r, tree_s, tree_r, sib_s, sib_r, tree2_s, tree2_r, sib2_s, sib2_r,
     swap_s, swap_r, part_s, part_r, sib3_s, sib3_r, grad_s, grad_r, fresh_s, fresh_r,
@@ -265,36 +266,138 @@
 
     inputs[:, columns_of(t)] = jnp.dot(choice[...], spread[...], preferred_element_type=F32).astype(BF16)
 
-    def input_view(chunk, low, count):
-        return inputs.at[pl.ds(low, count), columns_of(chunk)]
-
-    tree = Tree(input_view, place.tp_ids, place.tp_dev, tree_s, tree_r, TOK, 224)
-    sibs = Siblings(tree, input_view, TOK, place, sib_s, sib_r)
-    tree.begin()
-    sibs.start("me")
+    def half_rows(half, low=0, count=HALF):
+        return pl.ds(half * HALF + low, count)
+
+    class Rows:
+        def __init__(self, half):
+            def view(chunk, low, count):
+                return inputs.at[half_rows(half, low, count), columns_of(chunk)]
+
+            self.half, self.waiting = half, ["me"]
+            self.tree = Tree(view, place.tp_ids, place.tp_dev, tree_s, tree_r, HALF, 128, 13 * half)
+            self.sibs = Siblings(self.tree, view, HALF, place, sib_s, sib_r, 8 * half)
+            self.steps = self.tree.steps(self.whole)
+
+        def begin(self):
+            self.tree.begin()
+            self.sibs.start("me")
+
+        def multiplied(self):
+            name = self.waiting.pop(0)
+            self.sibs.wait(name)
+            at = half_rows(self.half)
+            depth = pl.ds(pl.multiple_of(self.tree.names[name] // 2 * (2 * SHARE), 2 * SHARE), 2 * SHARE)
+            for n in range(2):
+                cols = slice(n * 512, (n + 1) * 512)
+                part = jnp.dot(inputs[at, depth], weight[depth, cols], preferred_element_type=F32)
+                gates[at, cols] = part if name == "me" else gates[at, cols] + part
+
+        def whole(self, name):
+            self.sibs.start(name)
+            self.waiting.append(name)
+            if len(self.waiting) > 2:
+                self.multiplied()
+
+        def run(self, first, last):
+            for step in self.steps[first:last]:
+                step()
+
+        def finish(self):
+            while self.waiting:
+                self.multiplied()
+
+    def gate_rows(half, tall, cols, keep):
+        def rows(n, carry):
+            at = pl.ds(pl.multiple_of(half * HALF + n * tall, tall), tall)
+            gate = gates[at, cols] * SCALING
+            logistic = 1.0 / (1.0 + jnp.exp(-gate))
+            factors = upstream[at, cols].astype(F32) * act[at, cols].astype(F32)
+            keep(n * tall, (factors * logistic * (1.0 + gate * (1.0 - logistic))).astype(BF16))
+            return carry
+
+        lax.fori_loop(0, HALF // tall, rows, 0)
+
+    own_entry = holders_ref[0, t]
+    owners = []
+    for s in range(SEVEN):
+        owner = jnp.int32(0)
+        for other in range(TP):
+            owner = jnp.where(holders_ref[0, other] == t * SEVEN + s, other, owner)
+        owners.append(owner)
+
+    class Pieces:
+        def __init__(self, half):
+            buffer = later if half else early
+
+            def view(chunk, low, count):
+                return buffer.at[chunk, pl.ds(low, count), :]
+
+            self.half, self.buffer = half, buffer
+            self.tree = Tree(view, place.tp_ids, place.tp_dev, tree2_s, tree2_r, HALF, HALF, 13 * half)
+            self.sibs = Siblings(self.tree, view, HALF, place, sib2_s, sib2_r, 8 * half)
+            self.steps = self.tree.steps(self.sibs.start)
+
+        def begin(self):
+            def keep(low, value):
+                self.buffer[t, pl.ds(pl.multiple_of(low, 64), 64), :] = value
+
+            gate_rows(self.half, 64, slice(WIDE, NARROW), keep)
+            self.tree.begin()
+            self.sibs.start("me")
+
+        def wide(self):
+            def keep(low, value):
+                grad[pl.ds(pl.multiple_of(self.half * HALF + low, 16), 16), :] = value
+
+            gate_rows(self.half, 16, slice(0, WIDE), keep)
+
+        def run(self, first, last):
+            for step in self.steps[first:last]:
+                step()
+
+        def choose(self):
+            for name in ORDER:
+                self.sibs.wait(name)
+            at = slice(self.half * HALF, (self.half + 1) * HALF)
+            for s, owner in enumerate(owners):
+                cols = slice(s * UNIT, (s + 1) * UNIT)
+                grads[r, at, cols] = jnp.where(own_entry == -2, self.buffer[owner], grad[at, cols])
+
+    def gathered(chunk, first=False):
+        part = lax.dot_general(
+            parts[chunk], grads[chunk], (((0,), (0,)), ((), ())), preferred_element_type=F32
+        )
+        total[...] = part if first else total[...] + part
+
+    def grad_tree(half):
+        def view(chunk, low, count):
+            return grads.at[chunk, half_rows(half, low, count), :]
+
+        return Tree(view, place.rep_ids, place.rep_dev, grad_s, grad_r, HALF, 128, 13 * half)
+
+    rows_a, rows_b = Rows(0), Rows(1)
+    pieces_a, pieces_b = Pieces(0), Pieces(1)
+    gtree_a, gtree_b = grad_tree(0), grad_tree(1)
+
+    rows_a.begin()
     load_weight.wait()
-
-    def multiplied(name, first=False):
-        sibs.wait(name)
-        depth = pl.ds(pl.multiple_of(tree.names[name] // 2 * (2 * SHARE), 2 * SHARE), 2 * SHARE)
-        for n in range(2):
-            cols = slice(n * 512, (n + 1) * 512)
-            part = jnp.dot(inputs[:, depth], weight[depth, cols], preferred_element_type=F32)
-            gates[:, cols] = part if first else gates[:, cols] + part
-
-    waiting = ["me"]
-
-    def whole(name):
-        sibs.start(name)
-        waiting.append(name)
-        if len(waiting) > 2:
-            before = waiting.pop(0)
-            multiplied(before, before == "me")
-
-    for step in tree.steps(whole):
-        step()
-    for name in waiting:
-        multiplied(name)
+    rows_a.run(0, 3)
+    rows_b.begin()
+    rows_a.run(3, 8)
+    rows_a.finish()
+    for load in load_factors:
+        load.wait()
+    pieces_a.begin()
+    rows_b.run(0, 3)
+    pieces_a.wide()
+    pieces_a.run(0, 1)
+    rows_b.run(3, 5)
+    pieces_a.run(1, 3)
+    rows_b.run(5, 8)
+    rows_b.finish()
+    pieces_b.begin()
+    pieces_a.run(3, 8)
 
     mine_rows = pl.ds(pl.multiple_of(place.chip * PART, PART), PART)
     mine_cols = pl.ds(pl.multiple_of(place.core * SHARE, SHARE), SHARE)
@@ -312,37 +415,6 @@
 
     each(REP, lambda k: swap_to(k).start())
     own_swap = loading(9, inputs.at[mine_rows, columns_of(2 * r + place.core)], parts.at[r, mine_rows, mine_cols])
-
-    for load in load_factors:
-        load.wait()
-
-    def gate_rows(tall, cols, keep):
-        def rows(n, carry):
-            at = pl.ds(pl.multiple_of(n * tall, tall), tall)
-            gate = gates[at, cols] * SCALING
-            logistic = 1.0 / (1.0 + jnp.exp(-gate))
-            factors = upstream[at, cols].astype(F32) * act[at, cols].astype(F32)
-            keep(at, (factors * logistic * (1.0 + gate * (1.0 - logistic))).astype(BF16))
-            return carry
-
-        lax.fori_loop(0, TOK // tall, rows, 0)
-
-    def keep_piece(at, value):
-        pieces[t, at, :] = value
-
-    def keep_wide(at, value):
-        grad[at, :] = value
-
-    gate_rows(64, slice(WIDE, NARROW), keep_piece)
-
-    def piece_view(chunk, low, count):
-        return pieces.at[chunk, pl.ds(low, count), :]
-
-    tree2 = Tree(piece_view, place.tp_ids, place.tp_dev, tree2_s, tree2_r, TOK, TOK)
-    sibs2 = Siblings(tree2, piece_view, TOK, place, sib2_s, sib2_r)
-    tree2.begin()
-    sibs2.start("me")
-    gate_rows(16, slice(0, WIDE), keep_wide)
 
     def part_view(chunk, low, count):
         at, side = chunk // 2, chunk % 2
@@ -354,51 +426,40 @@
 
     ptree = Tree(part_view, place.tp_ids, place.tp_dev, part_s, part_r, REP, REP)
     sibs3 = Siblings(ptree, part_view, REP, place, sib3_s, sib3_r)
-    steps2 = tree2.steps(sibs2.start)
-    for step in steps2[:5]:
-        step()
+    psteps = ptree.steps(sibs3.start)
+    gsteps_a = gtree_a.steps(lambda name: None)
+    late = []
+    gsteps_b = gtree_b.steps(late.append)
+
+    def run(*steps):
+        for step in steps:
+            step()
+
+    pieces_a.choose()
+    gtree_a.begin()
+    pieces_b.wide()
+    pieces_b.run(0, 3)
     own_swap.wait()
     each(REP, lambda k: swap_from(k).wait_recv())
     ptree.begin()
     sibs3.start("me")
-    for step in steps2[5:]:
-        step()
-    for name in ORDER:
-        sibs2.wait(name)
-
-    own_entry = holders_ref[0, t]
-    for s in range(SEVEN):
-        wanted = t * SEVEN + s
-        owner = jnp.int32(0)
-        for other in range(TP):
-            owner = jnp.where(holders_ref[0, other] == wanted, other, owner)
-        cols = slice(s * UNIT, (s + 1) * UNIT)
-        grads[r, :, cols] = jnp.where(own_entry == -2, pieces[owner], grad[:, cols])
-
-    def grad_view(chunk, low, count):
-        return grads.at[chunk, pl.ds(low, count), :]
-
-    gtree = Tree(grad_view, place.rep_ids, place.rep_dev, grad_s, grad_r, TOK, 256)
-    gtree.begin()
-
-    def gathered(chunk, first=False):
-        part = lax.dot_general(
-            parts[chunk], grads[chunk], (((0,), (0,)), ((), ())), preferred_element_type=F32
-        )
-        total[...] = part if first else total[...] + part
-
+    pieces_b.run(3, 8)
+    run(*gsteps_a[:3])
+    pieces_b.choose()
+    gtree_b.begin()
     own_map.wait()
     each(REP, lambda k: map_from(k).wait_recv())
     load_maps = loading(10, maps_out, maps)
-    gsteps = gtree.steps(lambda name: gathered(gtree.names[name]))
-    for step in ptree.steps(sibs3.start):
-        step()
-    gsteps[0]()
+    run(*psteps[:3], *gsteps_a[3:5], *psteps[3:], gsteps_b[0], *gsteps_a[5:], *gsteps_b[1:3])
     for name in ORDER:
         sibs3.wait(name)
     gathered(r, True)
-    for step in gsteps[1:]:
+    for step in gsteps_b[3:]:
+        while late:
+            gathered(gtree_b.names[late.pop(0)])
         step()
+    while late:
+        gathered(gtree_b.names[late.pop(0)])
 
     for load in load_state:
         load.wait()
@@ -510,7 +571,10 @@
         step()
     each(REP, lambda k: three_from(k).wait_recv())
 
-    for book in (tree, sibs, tree2, sibs2, ptree, sibs3, gtree, ftree):
+    for part in (rows_a, rows_b, pieces_a, pieces_b):
+        part.tree.drain()
+        part.sibs.drain()
+    for book in (ptree, sibs3, gtree_a, gtree_b, ftree):
         book.drain()
     each(REP, lambda k: map_to(k).wait_send())
     each(TP, lambda k: share_to(k).wait_send())
@@ -589,7 +653,8 @@
             pltpu.VMEM((TOK, NARROW), BF16),
             pltpu.VMEM((TOK, NARROW), BF16),
             pltpu.VMEM((TOK, WIDE), BF16),
-            pltpu.VMEM((TP, TOK, UNIT), BF16),
+            pltpu.VMEM((TP, HALF, UNIT), BF16),
+            pltpu.VMEM((TP, HALF, UNIT), BF16),
             pltpu.VMEM((REP, TOK, ROWS), BF16),
             pltpu.VMEM((REP, TOK, WIDE), BF16),
             pltpu.VMEM((ROWS, WIDE), F32),
@@ -599,8 +664,8 @@
             pltpu.VMEM((KINDS, ROWS, UNIT), BF16),
             pltpu.VMEM((REP, ROWS, UNIT), BF16),
             pltpu.SMEM((REP, 1, TP), jnp.int32),
-            *sems(REP, TP, 13, 8, 13, 8),
-            *sems(REP, 13, 8, 13, 13, TP, TP, REP),
+            *sems(REP, TP, 26, 16, 26, 16),
+            *sems(REP, 13, 8, 26, 13, TP, TP, REP),
             pltpu.SemaphoreType.DMA((11,)),
         ],
         compiler_params=pltpu.CompilerParams(

time: 180 us -> 177 us (0.983)
  Pallas kernels: 178 us -> 176 us
    pallas_call x1, Pallas kernels: 173 us -> 171 us  [on_device(): pl.pallas_call(step_kernel, out_shape=(*(pltpu.VMEM(a.shape, a.dtype) for...]
where the time goes in v6:
time: 177 us; the launch traced here: 176 us
  Pallas kernels  176 us (99%)
    pallas_call x1, Pallas kernels, on_device(): pl.pallas_call(step_kernel, out_shape=(*(pltpu.VMEM(a.shape, a.dtype) for...  171 us
    pallas_call x1, Pallas kernels, on_device(): pl.pallas_call(finish_kernel, out_shape=(*state, jax.ShapeDtypeStruct((D,...  5.05 us

profile of v6, /device:TPU:0, one launch (start us, length us, event | category | flops | bytes accessed | tf_op | source)
XLA Modules:
  0.0 176.4 jit_solution(8785550374051518767)
XLA Ops:
  0.6 0.0 copy-start
  0.6 170.7 %step.1 = (f32[512,896]{1,0:T(8,128)S(1)}, bf16[512,896]{1,0:T(8,128)(2,1)S(1)}, bf16[512,896]{1,0:T(8,128)(2,1)S(1)}, bf16[8,512,896]{2,1,0:T(8,128)(2,1)S(1)},...) custom-call(bf16[96,4096]{1,0:T(8,128)(2,1)} %rows_ref.1, s32[1,384]{1,0:T(1,128)} %slots_ref.1, ...), custom_call_target="tpu_custom_call" | custom-call | tf_op jit(solution)/shard_map/step/pallas_call | solution.py:635
  171.3 0.0 copy-done
  171.3 5.1 %finish.1 = (f32[512,896]{1,0:T(8,128)}, bf16[512,896]{1,0:T(8,128)(2,1)}, bf16[512,896]{1,0:T(8,128)(2,1)}, bf16[4096,1024]{1,0:T(8,128)(2,1)}) custom-call(s32[1,16]{1,0:T(1,128)S(1)} %copy-done, f32[512,896]{1,0:T(8,128)S(1)} %get-tuple-element.9.master, bf16[512,896]{1,0:T(8,128)(2,1)S(1)} %get-tuple-element.10.one, ...), custom_call_target="tpu_custom_call" | custom-call | tf_op jit(solution)/shard_map/finish/pallas_call | solution.py:679
Async XLA Ops:
  0.6 170.7 %copy-start = (s32[1,16]{1,0:T(1,128)S(1)}, s32[1,16]{1,0:T(1,128)}, u32[]{:S(2)}) copy-start(s32[1,16]{1,0:T(1,128)} %holders_ref.3) | copy-start | bytes 196

commit v7 on v6

--- a/solution.py
+++ b/solution.py
@@ -550,7 +550,7 @@
     routed[:, strip_of(t), :] = picked[t]
 
     fsteps = ftree.steps(lambda name: None)
-    for step in fsteps[:3]:
+    for step in fsteps[:5]:
         step()
     each(TP, lambda k: two_from(k).wait_recv())
     for q in range(REP):
@@ -567,7 +567,7 @@
 
     each(REP, lambda k: three_to(k).start())
     adopted[r] = outgoing[r]
-    for step in fsteps[3:]:
+    for step in fsteps[5:]:
         step()
     each(REP, lambda k: three_from(k).wait_recv())
 
@@ -608,7 +608,7 @@
                 stage[to, cols] = jnp.where(failed, jnp.zeros_like(value), value)
             return carry
 
-        lax.fori_loop(0, ROWS // 32, rows, 0)
+        lax.fori_loop(0, ROWS // 32, rows, 0, unroll=4)
         span = pl.ds(chunk * ROWS, ROWS)
         storing(stage.at[span], copy_out.at[span])
     for store in stores:

time: 177 us -> 177 us (level)
  no operation moved by 1% of the time
where the time goes in v7:
time: 177 us; the launch traced here: 176 us
  Pallas kernels  176 us (99%)
    pallas_call x1, Pallas kernels, on_device(): pl.pallas_call(step_kernel, out_shape=(*(pltpu.VMEM(a.shape, a.dtype) for...  171 us
    pallas_call x1, Pallas kernels, on_device(): pl.pallas_call(finish_kernel, out_shape=(*state, jax.ShapeDtypeStruct((D,...  5.05 us

profile of v7, /device:TPU:0, one launch (start us, length us, event | category | flops | bytes accessed | tf_op | source)
XLA Modules:
  0.0 176.4 jit_solution(15968956373576763067)
XLA Ops:
  0.6 0.0 copy-start
  0.6 170.7 %step.1 = (f32[512,896]{1,0:T(8,128)S(1)}, bf16[512,896]{1,0:T(8,128)(2,1)S(1)}, bf16[512,896]{1,0:T(8,128)(2,1)S(1)}, bf16[8,512,896]{2,1,0:T(8,128)(2,1)S(1)},...) custom-call(bf16[96,4096]{1,0:T(8,128)(2,1)} %rows_ref.1, s32[1,384]{1,0:T(1,128)} %slots_ref.1, ...), custom_call_target="tpu_custom_call" | custom-call | tf_op jit(solution)/shard_map/step/pallas_call | solution.py:635
  171.3 0.0 copy-done
  171.3 5.1 %finish.1 = (f32[512,896]{1,0:T(8,128)}, bf16[512,896]{1,0:T(8,128)(2,1)}, bf16[512,896]{1,0:T(8,128)(2,1)}, bf16[4096,1024]{1,0:T(8,128)(2,1)}) custom-call(s32[1,16]{1,0:T(1,128)S(1)} %copy-done, f32[512,896]{1,0:T(8,128)S(1)} %get-tuple-element.9.master, bf16[512,896]{1,0:T(8,128)(2,1)S(1)} %get-tuple-element.10.one, ...), custom_call_target="tpu_custom_call" | custom-call | tf_op jit(solution)/shard_map/finish/pallas_call | solution.py:679
Async XLA Ops:
  0.6 170.7 %copy-start = (s32[1,16]{1,0:T(1,128)S(1)}, s32[1,16]{1,0:T(1,128)}, u32[]{:S(2)}) copy-start(s32[1,16]{1,0:T(1,128)} %holders_ref.3) | copy-start | bytes 196
